TPU v7x, 32 devices: a whole 2x2x4 slice. The times are simulated.
32 devices in a mesh: res: 8 (over z, y), mp: 4 (over x, core).
Axes of the slice: x: 2, y: 2, z: 4, core: 2. Of those that a mesh axis runs over, the one named last changes fastest.
Arguments:
- nodes: float32 [1536, 512], P('res'), may hold values from -6 to 6
- edges: float32 [1536, 6912], P('res'), may hold values from -6 to 6
- neighbours: int32 [1536, 36], P('res'), may hold values from 0 to 1535, as said below
- edge_mask: int32 [1536, 36], P('res'), may hold values from 0 to 1, as said below
- msg_in: bfloat16 [1216, 512], P(None, 'mp'), may hold values from -0.15625 to 0.15625
- msg_out: bfloat16 [512, 512], P('mp'), may hold values from -0.25 to 0.25
- gain_a: float32 [512], replicated, may hold values from 0.5 to 1.5
- ffn_in: bfloat16 [512, 2048], P(None, 'mp'), may hold values from -0.25 to 0.25
- ffn_out: bfloat16 [2048, 512], P('mp'), may hold values from -0.125 to 0.125
- gain_b: float32 [512], replicated, may hold values from 0.5 to 1.5
- edge_in: bfloat16 [1216, 768], P(None, 'mp'), may hold values from -0.15625 to 0.15625
- edge_out: bfloat16 [768, 192], P('mp'), may hold values from -0.21875 to 0.21875
- gain_c: float32 [192], replicated, may hold values from 0.5 to 1.5
- node_cot: float32 [1536, 512], P('res'), may hold values from -6 to 6
- edge_cot: float32 [1536, 6912], P('res'), may hold values from -6 to 6
Outputs:
- new_nodes: float32 [1536, 512], P('res')
- new_edges: float32 [1536, 6912], P('res')
- node_grad: float32 [1536, 512], P(('res', 'mp'))
- edge_grad: float32 [1536, 6912], P(('res', 'mp'))
- msg_in_grad: float32 [1216, 512], P(None, 'mp')
- msg_out_grad: float32 [512, 512], P('mp')
- gain_a_grad: float32 [512], replicated
- ffn_in_grad: float32 [512, 2048], P(None, 'mp')
- ffn_out_grad: float32 [2048, 512], P('mp')
- gain_b_grad: float32 [512], replicated
- edge_in_grad: float32 [1216, 768], P(None, 'mp')
- edge_out_grad: float32 [768, 192], P('mp')
- gain_c_grad: float32 [192], replicated
Inputs may be any that keep to these rules, and one draw needn't show every extreme that they name: `neighbours`: each edge of residue i leads to a residue at most 192 places from i, clamped to the residues that exist. `edge_mask`: some residues have all their edges 0.
All inputs are finite; a program needn't handle non-finite values.
Results may differ from a plain program's by a relative error of at most 0.024.
Values may be sent and summed in bfloat16 or wider, within the bound.
A program may use at most 128 MiB of HBM per device.

v0:
```python
import jax
import jax.numpy as jnp
from jax import lax
from jax.sharding import PartitionSpec as P

EPSILON = 1e-05
ROOT_HALF = 0.7071067811865476
ROOT_TWO_PI = 0.3989422804014327


def with_halo(value, sides, width):
    for axis, dim in sides:
        count, length = (lax.axis_size(axis), value.shape[dim])
        up = [(i, (i + 1) % count) for i in range(count - 1)]
        down = [(j, i) for i, j in up]
        last = lax.slice_in_dim(value, length - width, length, axis=dim)
        first = lax.slice_in_dim(value, 0, width, axis=dim)
        before = lax.ppermute(last, axis, up)
        after = lax.ppermute(first, axis, down)
        value = jnp.concatenate([before, value, after], axis=dim)
    return value


def product(left_side, right_side):
    return jnp.dot(left_side, right_side, preferred_element_type=jnp.float32)


def contract_rows(left_side, right_side):
    return lax.dot_general(
        left_side, right_side, (((0,), (0,)), ((), ())), preferred_element_type=jnp.float32
    )


def against(left_side, right_side):
    return lax.dot_general(
        left_side, right_side, (((1,), (1,)), ((), ())), preferred_element_type=jnp.float32
    )


def smooth(values):
    return jax.nn.gelu(values, approximate=False)


def smooth_slope(values):
    return (
        0.5 * (1.0 + lax.erf(values * ROOT_HALF))
        + values * jnp.exp(-0.5 * values * values) * ROOT_TWO_PI
    )


def norm_parts(values):
    centred = values - jnp.mean(values, axis=-1, keepdims=True)
    inverse = lax.rsqrt(jnp.mean(centred * centred, axis=-1, keepdims=True) + EPSILON)
    return (centred * inverse, inverse)


def norm_back(upstream, normed, inverse, norm_gain):
    scaled = upstream * norm_gain
    d_values = inverse * (
        scaled
        - jnp.mean(scaled, axis=-1, keepdims=True)
        - normed * jnp.mean(scaled * normed, axis=-1, keepdims=True)
    )
    return (d_values, jnp.sum(upstream * normed, axis=0))


def fetch_rows(low_states):
    return with_halo(low_states, (("res", 0),), low_states.shape[0])


def return_rows(extended):
    height = extended.shape[0] // 3
    outward = jnp.concatenate([extended[:height], extended[2 * height :]], axis=0)
    arrived = with_halo(outward.astype(jnp.bfloat16), (("res", 0),), height).astype(outward.dtype)
    return extended[height : 2 * height] + arrived[:height] + arrived[3 * height :]


def model_sum(values):
    return lax.psum(values.astype(jnp.bfloat16), "mp").astype(jnp.float32)


def edge_total(values):
    return lax.psum(values.astype(jnp.bfloat16), "mp").astype(jnp.float32)


def unchanged(values):
    return values


def neighbour_terms(own_low, low_states, self_weight, other_weight, local_index, degree):
    count = own_low.shape[0]
    extended = fetch_rows(low_states)
    self_term = product(own_low, self_weight)
    other_term = jnp.take(product(extended, other_weight), local_index, axis=0).reshape(
        count, degree, -1
    )
    return (self_term[:, None, :] + other_term).reshape(count * degree, -1)


def neighbour_back(
    d_before, own_low, low_states, self_weight, other_weight, local_index, degree, finish
):
    count = own_low.shape[0]
    height = low_states.shape[0]
    d_float = d_before.astype(jnp.float32)
    d_self = jnp.sum(d_float.reshape(count, degree, -1), axis=1).astype(jnp.bfloat16)
    d_other = finish(
        return_rows(jax.ops.segment_sum(d_float, local_index, num_segments=3 * height))
    ).astype(jnp.bfloat16)
    gradients = (contract_rows(own_low, d_self), contract_rows(own_low, d_other))
    node_part = against(d_self, self_weight) + against(d_other, other_weight)
    return (gradients, node_part)


def node_tail(states, gathered, gain_a, ffn_in, ffn_out, gain_b):
    normed_a, inverse_a = norm_parts(states + gathered)
    middle = normed_a * gain_a
    middle_low = middle.astype(jnp.bfloat16)
    hidden = product(middle_low, ffn_in)
    smooth_low = smooth(hidden).astype(jnp.bfloat16)
    update = model_sum(product(smooth_low, ffn_out))
    normed_b, inverse_b = norm_parts(middle + update)
    return (
        normed_b * gain_b,
        (normed_a, inverse_a, middle_low, hidden, smooth_low, normed_b, inverse_b),
    )


def tail_back(d_out, saved, gain_a, ffn_in, ffn_out, gain_b):
    normed_a, inverse_a, middle_low, hidden, smooth_low, normed_b, inverse_b = saved
    d_sum_b, g_gain_b = norm_back(d_out, normed_b, inverse_b, gain_b)
    d_ffn = d_sum_b.astype(jnp.bfloat16)
    g_ffn_out = contract_rows(smooth_low, d_ffn)
    d_hidden = (against(d_ffn, ffn_out) * smooth_slope(hidden)).astype(jnp.bfloat16)
    g_ffn_in = contract_rows(middle_low, d_hidden)
    d_middle = d_sum_b + model_sum(against(d_hidden, ffn_in))
    d_sum_a, g_gain_a = norm_back(d_middle, normed_a, inverse_a, gain_a)
    return (d_sum_a, (g_gain_a, g_ffn_in, g_ffn_out, g_gain_b))


def node_pass(states, own_rows, edge_low, local_index, weights_mean, weights, finish):
    msg_self, msg_other, msg_edge, msg_out, gain_a, ffn_in, ffn_out, gain_b = weights
    degree = weights_mean.shape[1]
    low_states = states.astype(jnp.bfloat16)
    own_low = own_rows(low_states)
    count = own_low.shape[0]
    before = neighbour_terms(
        own_low, low_states, msg_self, msg_other, local_index, degree
    ) + product(edge_low, msg_edge)
    before = before.reshape(count, degree, -1)
    averaged_low = jnp.sum(smooth(before) * weights_mean[:, :, None], axis=1).astype(jnp.bfloat16)
    gathered = finish(product(averaged_low, msg_out))
    result, tail_saved = node_tail(states, gathered, gain_a, ffn_in, ffn_out, gain_b)
    return (result, (low_states, own_low, before, averaged_low, tail_saved))


def edge_pass(edge_states, base_term, edge_edge, edge_out, gain_c, finish):
    edge_low = edge_states.astype(jnp.bfloat16)
    before = base_term + product(edge_low, edge_edge)
    smooth_low = smooth(before).astype(jnp.bfloat16)
    update = finish(product(smooth_low, edge_out))
    normed, inverse = norm_parts(edge_states + update)
    return (normed * gain_c, (edge_low, before, smooth_low, normed, inverse))


def run_layer(
    nodes,
    edge_flat,
    local_index,
    weights_mean,
    msg_in,
    msg_out,
    gain_a,
    ffn_in,
    ffn_out,
    gain_b,
    edge_in,
    edge_out,
    gain_c,
    node_cot,
    edge_cot_flat,
    own_rows,
    message_finish,
    edge_finish,
    row_finish,
    part_finish,
):
    node_width = nodes.shape[1]
    degree = weights_mean.shape[1]
    edge_low = edge_flat.astype(jnp.bfloat16)
    msg_self = msg_in[:node_width]
    msg_other = msg_in[node_width : 2 * node_width]
    msg_edge = msg_in[2 * node_width :]
    edge_self = edge_in[:node_width]
    edge_other = edge_in[node_width : 2 * node_width]
    edge_edge = edge_in[2 * node_width :]
    node_weights = (msg_self, msg_other, msg_edge, msg_out, gain_a, ffn_in, ffn_out, gain_b)
    predicted, unused_first = node_pass(
        nodes, own_rows, edge_low, local_index, weights_mean, node_weights, message_finish
    )
    mixed = 0.5 * (nodes + predicted)
    settled, node_saved = node_pass(
        mixed, own_rows, edge_low, local_index, weights_mean, node_weights, message_finish
    )
    settled_low = settled.astype(jnp.bfloat16)
    own_settled = own_rows(settled_low)
    base_term = neighbour_terms(
        own_settled, settled_low, edge_self, edge_other, local_index, degree
    )
    guess, unused_second = edge_pass(edge_flat, base_term, edge_edge, edge_out, gain_c, edge_finish)
    edge_mixed = 0.5 * (edge_flat + guess)
    new_edge_flat, edge_saved = edge_pass(
        edge_mixed, base_term, edge_edge, edge_out, gain_c, edge_finish
    )
    mixed_low, before_edge, smooth_edge, normed_c, inverse_c = edge_saved
    d_edge_sum, g_gain_c = norm_back(edge_cot_flat, normed_c, inverse_c, gain_c)
    d_update = d_edge_sum.astype(jnp.bfloat16)
    g_edge_out = contract_rows(smooth_edge, d_update)
    d_before_edge = (against(d_update, edge_out) * smooth_slope(before_edge)).astype(jnp.bfloat16)
    g_edge_edge = contract_rows(mixed_low, d_before_edge)
    (g_edge_self, g_edge_other), settled_part = neighbour_back(
        d_before_edge,
        own_settled,
        settled_low,
        edge_self,
        edge_other,
        local_index,
        degree,
        row_finish,
    )
    edge_mix_part = against(d_before_edge, edge_edge)
    d_settled = node_cot + part_finish(settled_part)
    low_states, own_low, before_node, averaged_low, tail_saved = node_saved
    count = own_low.shape[0]
    d_sum_a, tail_grads = tail_back(d_settled, tail_saved, gain_a, ffn_in, ffn_out, gain_b)
    g_gain_a, g_ffn_in, g_ffn_out, g_gain_b = tail_grads
    d_gathered = own_rows(d_sum_a).astype(jnp.bfloat16)
    g_msg_out = contract_rows(averaged_low, d_gathered)
    d_averaged = against(d_gathered, msg_out)
    d_before_node = (
        (d_averaged[:, None, :] * weights_mean[:, :, None] * smooth_slope(before_node))
        .reshape(count * degree, -1)
        .astype(jnp.bfloat16)
    )
    g_msg_edge = contract_rows(edge_low, d_before_node)
    (g_msg_self, g_msg_other), mixed_part = neighbour_back(
        d_before_node, own_low, low_states, msg_self, msg_other, local_index, degree, row_finish
    )
    edge_part = 0.5 * edge_mix_part + against(d_before_node, msg_edge)
    msg_in_grad = jnp.concatenate([g_msg_self, g_msg_other, g_msg_edge], axis=0)
    edge_in_grad = jnp.concatenate([g_edge_self, g_edge_other, g_edge_edge], axis=0)
    gradients = (
        msg_in_grad,
        g_msg_out,
        g_gain_a,
        g_ffn_in,
        g_ffn_out,
        g_gain_b,
        edge_in_grad,
        g_edge_out,
        g_gain_c,
    )
    return (settled, new_edge_flat, d_sum_a, mixed_part, d_edge_sum, edge_part, gradients)


def on_device(
    nodes,
    edges,
    neighbours,
    edge_mask,
    msg_in,
    msg_out,
    gain_a,
    ffn_in,
    ffn_out,
    gain_b,
    edge_in,
    edge_out,
    gain_c,
    node_cot,
    edge_cot,
):
    height = nodes.shape[0]
    degree = neighbours.shape[1]
    edge_count = height * degree
    local_index = (neighbours - (lax.axis_index("res") - 1) * height).reshape(-1)
    live_edges = edge_mask.astype(jnp.float32)
    weights_mean = live_edges / jnp.maximum(jnp.sum(live_edges, axis=1, keepdims=True), 1.0)
    position = lax.axis_index("mp")
    edge_flat = edges.reshape(edge_count, -1)
    settled, new_edge_flat, d_sum_a, mixed_part, d_edge_sum, edge_part, gradients = run_layer(
        nodes,
        edge_flat,
        local_index,
        weights_mean,
        msg_in,
        msg_out,
        gain_a,
        ffn_in,
        ffn_out,
        gain_b,
        edge_in,
        edge_out,
        gain_c,
        node_cot,
        edge_cot.reshape(edge_count, -1),
        unchanged,
        model_sum,
        edge_total,
        unchanged,
        model_sum,
    )
    share_nodes, share_edges = (
        lax.psum_scatter(
            mixed_part.astype(jnp.bfloat16), "mp", scatter_dimension=0, tiled=True
        ).astype(jnp.float32),
        lax.psum_scatter(
            edge_part.astype(jnp.bfloat16), "mp", scatter_dimension=0, tiled=True
        ).astype(jnp.float32),
    )
    node_piece = share_nodes.shape[0]
    edge_piece = share_edges.shape[0]
    node_grad = 0.5 * (
        lax.dynamic_slice_in_dim(d_sum_a, position * node_piece, node_piece, 0) + share_nodes
    )
    edge_grad = (
        0.5 * lax.dynamic_slice_in_dim(d_edge_sum, position * edge_piece, edge_piece, 0)
        + share_edges
    )
    (
        msg_in_grad,
        g_msg_out,
        g_gain_a,
        g_ffn_in,
        g_ffn_out,
        g_gain_b,
        edge_in_grad,
        g_edge_out,
        g_gain_c,
    ) = gradients
    summed = lax.psum(
        (
            msg_in_grad,
            g_msg_out,
            g_gain_a,
            g_ffn_in,
            g_ffn_out,
            g_gain_b,
            edge_in_grad,
            g_edge_out,
            g_gain_c,
        ),
        "res",
    )
    return (
        settled,
        new_edge_flat.reshape(height, -1),
        node_grad,
        edge_grad.reshape(node_piece, -1),
        summed[0],
        summed[1],
        summed[2],
        summed[3],
        summed[4],
        summed[5],
        summed[6],
        summed[7],
        summed[8],
    )


def solution(mesh):
    in_specs = (
        P("res", None),
        P("res", None),
        P("res", None),
        P("res", None),
        P(None, "mp"),
        P("mp", None),
        P(),
        P(None, "mp"),
        P("mp", None),
        P(),
        P(None, "mp"),
        P("mp", None),
        P(),
        P("res", None),
        P("res", None),
    )
    out_specs = (
        P("res", None),
        P("res", None),
        P(("res", "mp"), None),
        P(("res", "mp"), None),
        P(None, "mp"),
        P("mp", None),
        P(),
        P(None, "mp"),
        P("mp", None),
        P(),
        P(None, "mp"),
        P("mp", None),
        P(),
    )
    return jax.shard_map(
        on_device, mesh=mesh, in_specs=in_specs, out_specs=out_specs, check_vma=False
    )
```

profile of v0, /device:TPU:0, one launch (start us, length us, event | category | flops | bytes accessed | tf_op | source)
XLA Modules:
  0.0 979.9 jit_solution(14811499099278638909)
XLA Ops:
  9.6 5.5 collective-permute-start
  21.2 4.6 add.247
  25.8 8.2 reshape.227
  34.0 5.9 fusion.193
  40.2 13.5 %gather_fusion.1 = f32[6912,128]{1,0:T(8,128)} fusion(f32[576,128]{1,0:T(8,128)S(1)} %fusion.68, s32[7168]{0:T(1024)S(1)} %pad_clamp_fusion.1), kind=kCustom, calls=%fused_computation.clone | custom fusion | bytes 7105536 | tf_op jit(solution)/shard_map/jit(_take)/gather | solution.py:94
  53.7 9.3 negate_multiply_fusion.3
  63.1 4.6 mul.406
  76.2 10.2 %fusion.30 = bf16[192,128]{1,0:T(8,128)(2,1)S(1)} fusion(f32[192,36,128]{2,1,0:T(8,128)} %mul.404, f32[192,36,128]{2,1,0:T(8,128)} %mul.406, f32[192,36]{1,0:T(8,128)S(1)} %copy.48), kind=kLoop, calls=%fused_computation.75 | loop fusion | flops 55713792 | bytes 7154688 | tf_op jit(solution)/shard_map/reduce_sum | solution.py:151
  87.4 33.4 %all-reduce.12.cloned.1.call-done = bf16[192,512]{1,0:T(8,128)(2,1)} async-done(((bf16[192,512]{1,0:T(8,128)(2,1)}), bf16[192,512]{1,0:T(8,128)(2,1)}) %all-reduce.12.cloned.1.call-update) | async-done | bytes 196624 | tf_op jit(solution)/shard_map/psum | solution.py:79
  126.3 31.7 %all-reduce.14.cloned.1.call-done = bf16[192,512]{1,0:T(8,128)(2,1)} async-done(((bf16[192,512]{1,0:T(8,128)(2,1)}), bf16[192,512]{1,0:T(8,128)(2,1)}) %all-reduce.14.cloned.1.call-update) | async-done | bytes 196624 | tf_op jit(solution)/shard_map/psum | solution.py:79
  160.8 4.8 collective-permute-start.2
  168.0 4.6 add.256
  172.9 13.5 %gather_fusion.2 = f32[6912,128]{1,0:T(8,128)} fusion(f32[576,128]{1,0:T(8,128)S(1)} %fusion.74, s32[7168]{0:T(1024)S(1)} %pad_clamp_fusion.1), kind=kCustom, calls=%fused_computation.1.clone | custom fusion | bytes 7105536 | tf_op jit(solution)/shard_map/jit(_take)/gather | solution.py:94
  186.4 9.3 negate_multiply_fusion.2
  195.8 4.6 mul.427
  208.9 10.2 %fusion.34 = bf16[192,128]{1,0:T(8,128)(2,1)S(1)} fusion(f32[192,36,128]{2,1,0:T(8,128)} %mul.425, f32[192,36,128]{2,1,0:T(8,128)} %mul.427, f32[192,36]{1,0:T(8,128)S(1)} %copy.48), kind=kLoop, calls=%fused_computation.79 | loop fusion | flops 55713792 | bytes 7154688 | tf_op jit(solution)/shard_map/reduce_sum | solution.py:151
  220.1 31.7 %all-reduce.16.cloned.1.call-done = bf16[192,512]{1,0:T(8,128)(2,1)} async-done(((bf16[192,512]{1,0:T(8,128)(2,1)}), bf16[192,512]{1,0:T(8,128)(2,1)}) %all-reduce.16.cloned.1.call-update) | async-done | bytes 196624 | tf_op jit(solution)/shard_map/psum | solution.py:79
  256.7 31.8 %all-reduce.18.cloned.1.call-done = bf16[192,512]{1,0:T(8,128)(2,1)} async-done(((bf16[192,512]{1,0:T(8,128)(2,1)}), bf16[192,512]{1,0:T(8,128)(2,1)}) %all-reduce.18.cloned.1.call-update) | async-done | bytes 196624 | tf_op jit(solution)/shard_map/psum | solution.py:79
  292.7 4.8 collective-permute-start.4
  301.3 8.7 add.264
  310.0 7.8 copy.52
  318.2 17.2 %gather_fusion = f32[6912,192]{1,0:T(8,128)} fusion(f32[576,192]{1,0:T(8,128)S(1)} %fusion.80, s32[7168]{0:T(1024)S(1)} %pad_clamp_fusion), kind=kCustom, calls=%fused_computation.2 | custom fusion | bytes 10644480 | tf_op jit(solution)/shard_map/jit(_take)/gather | solution.py:94
  335.4 7.9 copy.51
  343.3 17.6 %convolution_convert_fusion.1 = bf16[6912,192]{0,1:T(8,128)(2,1)} fusion(bf16[192,192]{1,0:T(8,128)(2,1)S(1)} %copy-done.44, f32[6912,192]{0,1:T(8,128)} %copy.52, f32[6912,192]{0,1:T(8,128)} %copy.51, pred[6912]{0:T(1024)(128)(4,1)S(1)} %compare_and_fusion, bf16[1216,192]{0,1:T(8,128)(2,1)S(1)} %copy-done.27, f32[6912,192]{1,0:T(8,128)} %reshape.227), kind=kOutput, calls=%fused_computation.13 | convolution fusion | flops 1112113152 | bytes 18783232 | tf_op jit(solution)/shard_map/dot_general | solution.py:25
  361.5 8.0 copy.54
  369.5 52.1 %all-reduce.20.cloned.1.call-done = bf16[6912,192]{0,1:T(8,128)(2,1)} async-done(((bf16[6912,192]{0,1:T(8,128)(2,1)}), bf16[6912,192]{0,1:T(8,128)(2,1)}) %all-reduce.20.cloned.1.call-update) | async-done | bytes 2654224 | tf_op jit(solution)/shard_map/psum | solution.py:83
  429.7 15.9 %fusion.7 = (bf16[6912,192]{0,1:T(8,128)(2,1)S(1)}, f32[6912,192]{0,1:T(8,128)}) fusion(f32[6912,192]{0,1:T(8,128)S(1)} %copy-done.1, f32[192]{0:T(256)S(1)} %copy-done.60, f32[6912]{0:T(1024)S(1)} %add_rsqrt_fusion.1, f32[6912]{0:T(1024)S(1)} %broadcast_multiply_fusion.5, bf16[6912,192]{0,1:T(8,128)(2,1)S(1)} %copy-done.3, bf16[1216,192]{0,1:T(8,128)(2,1)} %param.27, ...), kind=kOutput, calls=%fused_computation.24 | convolution fusion | flops 610467840 | bytes 26703360 | tf_op jit(solution)/shard_map/dot_general | solution.py:25
  449.8 8.2 reshape.230
  458.0 7.9 copy.56
  465.8 44.4 %all-reduce.22.cloned.1.call-done = bf16[6912,192]{0,1:T(8,128)(2,1)} async-done(((bf16[6912,192]{0,1:T(8,128)(2,1)}), bf16[6912,192]{0,1:T(8,128)(2,1)}) %all-reduce.22.cloned.1.call-update) | async-done | bytes 2654224 | tf_op jit(solution)/shard_map/psum | solution.py:83
  519.9 5.6 subtract_multiply_fusion
  525.5 6.7 fusion.1
  532.2 4.7 copy.57
  536.9 8.6 reshape.231
  545.5 36.4 %scatter_custom_fusion = f32[576,192]{1,0:T(8,128)} fusion(s32[6912]{0:T(1024)} %copy-done.40, f32[6912,192]{1,0:T(8,128)} %copy.57, f32[]{:T(128)} %constant.69.clone.1), kind=kCustom, calls=%fused_computation.229 | custom fusion | flops 1327104 | bytes 442880 | tf_op jit(solution)/shard_map/scatter-add | solution.py:108
  598.1 33.0 %all-reduce.24.cloned.1.call-done = bf16[192,512]{1,0:T(8,128)(2,1)} async-done(((bf16[192,512]{1,0:T(8,128)(2,1)}), bf16[192,512]{1,0:T(8,128)(2,1)}) %all-reduce.24.cloned.1.call-update) | async-done | bytes 196624 | tf_op jit(solution)/shard_map/psum | solution.py:79
  642.6 27.7 %all-reduce.26.cloned.1.call-done = bf16[192,512]{1,0:T(8,128)(2,1)} async-done(((bf16[192,512]{1,0:T(8,128)(2,1)}), bf16[192,512]{1,0:T(8,128)(2,1)}) %all-reduce.26.cloned.1.call-update) | async-done | bytes 196624 | tf_op jit(solution)/shard_map/psum | solution.py:79
  676.0 4.6 mul.492
  680.6 5.3 fusion.52
  685.9 36.8 %scatter_custom_fusion.1 = f32[576,128]{1,0:T(8,128)S(1)} fusion(s32[6912]{0:T(1024)} %copy-done.40, bf16[6912,128]{1,0:T(8,128)(2,1)S(1)} %fusion.52, f32[]{:T(128)} %constant.69.clone.1), kind=kCustom, calls=%fused_computation.141 | custom fusion | flops 1769472 | bytes 2064896 | tf_op jit(solution)/shard_map/scatter-add | solution.py:108
  738.4 4.8 fusion
  743.2 5.6 copy.63
  749.5 5.0 fusion.57
  754.5 5.2 fusion.60
  767.5 8.0 copy.55
  775.5 8.3 reshape.229
  783.8 20.8 %all-reduce = (f32[512]{0:T(512)}, f32[512]{0:T(512)}, f32[192]{0:T(256)}) all-reduce(f32[512]{0:T(512)S(1)} %copy-done.63, f32[512]{0:T(512)S(1)} %copy-done.62, f32[192]{0:T(256)S(1)} %copy-done.64), channel_id=1, replica_groups=mesh['res'=8,'mp'=4] {'res'}, use_global_device_ids=true, to_apply=%region_38.40 | all-reduce | flops 1216 | bytes 9728 | tf_op jit(solution)/shard_map/psum | solution.py:341
  814.2 150.1 %all-reduce.28.cloned.1.call-done = (f32[1216,128]{1,0:T(8,128)}, f32[128,512]{1,0:T(8,128)}, f32[512,512]{1,0:T(8,128)}, f32[512,512]{1,0:T(8,128)}, f32[1216,192]{0,1:T(8,128)}, /*index=5*/f32[192,192]{1,0:T(8,128)}) async-done(((f32[1216,128]{1,0:T(8,128)}, f32[128,512]{1,0:T(8,128)}, f32[512,512]{1,0:T(8,128)}, f32[512,512]{1,0:T(8,128)}, f32[1216,192]{0,1:T(8,128)}, /*index=5*/f32[192,192]{1,0:T(8,128)}), ...) | async-done | bytes 4063248 | tf_op jit(solution)/shard_map/psum | solution.py:341
  (285 shorter events, 149.5 us)
Async XLA Ops:
  7.2 115.8 %copy-start = (bf16[512,512]{1,0:T(8,128)(2,1)S(1)}, bf16[512,512]{1,0:T(8,128)(2,1)}, u32[]{:S(2)}) copy-start(bf16[512,512]{1,0:T(8,128)(2,1)} %param.24) | copy-start | bytes 1572868
  7.2 113.6 %all-reduce.12.cloned.1.call-start = ((), (), s32[]{:S(2)}) async-start(), calls=%async_computation.2 | async-start | bytes 393216 | tf_op jit(solution)/shard_map/psum | solution.py:79
  8.3 31.6 %collective-permute-start.1 = (bf16[192,512]{1,0:T(8,128)(2,1)S(1)}, bf16[192,512]{1,0:T(8,128)(2,1)S(1)}, u32[]{:S(2)}, u32[]{:S(2)}) collective-permute-start(bf16[192,512]{1,0:T(8,128)(2,1)S(1)} %convert_element_type.147), channel_id=1, source_target_pairs={{4,0},{8,4},{12,8},{16,12},{20,16},{24,20},{28,24},{5,1},{9,5},{13... | collective-permute-start | bytes 589832 | tf_op jit(solution)/shard_map/ppermute | solution.py:19
  9.6 30.3 %collective-permute-start = (bf16[192,512]{1,0:T(8,128)(2,1)S(1)}, bf16[192,512]{1,0:T(8,128)(2,1)S(1)}, u32[]{:S(2)}, u32[]{:S(2)}) collective-permute-start(bf16[192,512]{1,0:T(8,128)(2,1)S(1)} %convert_element_type.147), channel_id=1, source_target_pairs={{0,4},{4,8},{8,12},{12,16},{16,20},{20,24},{24,28},{1,5},{5,9},{9,... | collective-permute-start | bytes 589832 | tf_op jit(solution)/shard_map/ppermute | solution.py:18
  16.8 192.1 %copy-start.19 = (f32[192,36]{1,0:T(8,128)}, f32[192,36]{1,0:T(8,128)S(1)}, u32[]{:S(2)}) copy-start(f32[192,36]{1,0:T(8,128)S(1)} %copy.48) | copy-start | bytes 82948
  17.9 21.9 %copy-start.40 = (s32[6912]{0:T(1024)}, s32[6912]{0:T(1024)S(1)}, u32[]{:S(2)}) copy-start(s32[6912]{0:T(1024)S(1)} %reshape.226) | copy-start | bytes 82948
  76.2 44.6 %copy-start.7 = (f32[192,512]{1,0:T(8,128)S(1)}, f32[192,512]{1,0:T(8,128)}, u32[]{:S(2)}) copy-start(f32[192,512]{1,0:T(8,128)} %param.17) | copy-start | bytes 1179652
  76.2 46.8 %copy-start.32 = (bf16[512,512]{1,0:T(8,128)(2,1)S(1)}, bf16[512,512]{1,0:T(8,128)(2,1)}, u32[]{:S(2)}) copy-start(bf16[512,512]{1,0:T(8,128)(2,1)} %param.25) | copy-start | bytes 1572868
  76.2 46.8 %copy-start.47 = (f32[512]{0:T(512)S(1)}, f32[512]{0:T(512)}, u32[]{:S(2)}) copy-start(f32[512]{0:T(512)} %param.23) | copy-start | bytes 6148
  87.4 70.6 %all-reduce.14.cloned.1.call-start = ((), (), s32[]{:S(2)}) async-start(), calls=%async_computation.3 | async-start | bytes 393216 | tf_op jit(solution)/shard_map/psum | solution.py:79
  123.1 34.9 %copy-start.18 = (bf16[192,512]{1,0:T(8,128)(2,1)S(1)}, bf16[192,512]{1,0:T(8,128)(2,1)}, u32[]{:S(2)}) copy-start(bf16[192,512]{1,0:T(8,128)(2,1)} %all-reduce.12.cloned.1.call-done) | copy-start | bytes 589828
  123.1 36.3 %copy-start.45 = (f32[512]{0:T(512)S(1)}, f32[512]{0:T(512)}, u32[]{:S(2)}) copy-start(f32[512]{0:T(512)} %param.26) | copy-start | bytes 6148
  126.1 125.7 %all-reduce.16.cloned.1.call-start = ((), (), s32[]{:S(2)}) async-start(), calls=%async_computation.4 | async-start | bytes 393216 | tf_op jit(solution)/shard_map/psum | solution.py:79
  159.5 13.1 %copy-start.14 = (bf16[192,512]{1,0:T(8,128)(2,1)}, bf16[192,512]{1,0:T(8,128)(2,1)S(1)}, u32[]{:S(2)}) copy-start(bf16[192,512]{1,0:T(8,128)(2,1)S(1)} %fusion.270) | copy-start | bytes 589828
  159.5 13.0 %collective-permute-start.3 = (bf16[192,512]{1,0:T(8,128)(2,1)S(1)}, bf16[192,512]{1,0:T(8,128)(2,1)S(1)}, u32[]{:S(2)}, u32[]{:S(2)}) collective-permute-start(bf16[192,512]{1,0:T(8,128)(2,1)S(1)} %fusion.270), channel_id=1, source_target_pairs={{4,0},{8,4},{12,8},{16,12},{20,16},{24,20},{28,24},{5,1},{9,5},{13... | collective-permute-start | bytes 589832 | tf_op jit(solution)/shard_map/ppermute | solution.py:19
  160.8 11.7 %collective-permute-start.2 = (bf16[192,512]{1,0:T(8,128)(2,1)S(1)}, bf16[192,512]{1,0:T(8,128)(2,1)S(1)}, u32[]{:S(2)}, u32[]{:S(2)}) collective-permute-start(bf16[192,512]{1,0:T(8,128)(2,1)S(1)} %fusion.270), channel_id=1, source_target_pairs={{0,4},{4,8},{8,12},{12,16},{16,20},{20,24},{24,28},{1,5},{5,9},{9,... | collective-permute-start | bytes 589832 | tf_op jit(solution)/shard_map/ppermute | solution.py:18
  220.0 68.6 %all-reduce.18.cloned.1.call-start = ((), (), s32[]{:S(2)}) async-start(), calls=%async_computation.5 | async-start | bytes 393216 | tf_op jit(solution)/shard_map/psum | solution.py:79
  253.0 35.5 %copy-start.8 = (f32[192,512]{1,0:T(8,128)}, f32[192,512]{1,0:T(8,128)S(1)}, u32[]{:S(2)}) copy-start(f32[192,512]{1,0:T(8,128)S(1)} %get-tuple-element.39) | copy-start | bytes 1179652
  253.0 35.5 %copy-start.50 = (f32[192]{0:T(256)}, f32[192]{0:T(256)S(1)}, u32[]{:S(2)}) copy-start(f32[192]{0:T(256)S(1)} %broadcast_multiply_fusion.11) | copy-start | bytes 2308
  253.2 35.3 %copy-start.53 = (f32[192]{0:T(256)}, f32[192]{0:T(256)S(1)}, u32[]{:S(2)}) copy-start(f32[192]{0:T(256)S(1)} %add_rsqrt_fusion.3) | copy-start | bytes 2308
  253.3 44.2 %copy-start.27 = (bf16[1216,192]{0,1:T(8,128)(2,1)S(1)}, bf16[1216,192]{0,1:T(8,128)(2,1)}, u32[]{:S(2)}) copy-start(bf16[1216,192]{0,1:T(8,128)(2,1)} %param.27) | copy-start | bytes 1400836
  256.7 164.9 %all-reduce.20.cloned.1.call-start = ((), (), s32[]{:S(2)}) async-start(), calls=%async_computation.6 | async-start | bytes 5308416 | tf_op jit(solution)/shard_map/psum | solution.py:83
  291.4 26.5 %copy-start.16 = (bf16[192,512]{1,0:T(8,128)(2,1)}, bf16[192,512]{1,0:T(8,128)(2,1)S(1)}, u32[]{:S(2)}) copy-start(bf16[192,512]{1,0:T(8,128)(2,1)S(1)} %get-tuple-element.34) | copy-start | bytes 589828
  291.4 26.5 %collective-permute-start.5 = (bf16[192,512]{1,0:T(8,128)(2,1)S(1)}, bf16[192,512]{1,0:T(8,128)(2,1)S(1)}, u32[]{:S(2)}, u32[]{:S(2)}) collective-permute-start(bf16[192,512]{1,0:T(8,128)(2,1)S(1)} %get-tuple-element.34), channel_id=1, source_target_pairs={{4,0},{8,4},{12,8},{16,12},{20,16},{24,20},{28,24},{5,1},{9,5},{13... | collective-permute-start | bytes 589832 | tf_op jit(solution)/shard_map/ppermute | solution.py:19
  292.7 25.2 %collective-permute-start.4 = (bf16[192,512]{1,0:T(8,128)(2,1)S(1)}, bf16[192,512]{1,0:T(8,128)(2,1)S(1)}, u32[]{:S(2)}, u32[]{:S(2)}) collective-permute-start(bf16[192,512]{1,0:T(8,128)(2,1)S(1)} %get-tuple-element.34), channel_id=1, source_target_pairs={{0,4},{4,8},{8,12},{12,16},{16,20},{20,24},{24,28},{1,5},{5,9},{9,... | collective-permute-start | bytes 589832 | tf_op jit(solution)/shard_map/ppermute | solution.py:18
  361.0 149.3 %all-reduce.22.cloned.1.call-start = ((), (), s32[]{:S(2)}) async-start(), calls=%async_computation.7 | async-start | bytes 5308416 | tf_op jit(solution)/shard_map/psum | solution.py:83
  427.2 83.0 %copy-start.38 = (f32[6912]{0:T(1024)}, f32[6912]{0:T(1024)S(1)}, u32[]{:S(2)}) copy-start(f32[6912]{0:T(1024)S(1)} %broadcast_multiply_fusion.5) | copy-start | bytes 82948
  429.7 80.5 %copy-start.42 = (f32[6912]{0:T(1024)}, f32[6912]{0:T(1024)S(1)}, u32[]{:S(2)}) copy-start(f32[6912]{0:T(1024)S(1)} %add_rsqrt_fusion.1) | copy-start | bytes 82948
  449.5 181.5 %all-reduce.24.cloned.1.call-start = ((), (), s32[]{:S(2)}) async-start(), calls=%async_computation.8 | async-start | bytes 393216 | tf_op jit(solution)/shard_map/psum | solution.py:79
  532.2 106.3 %copy-start.6 = (bf16[6912,192]{0,1:T(8,128)(2,1)}, bf16[6912,192]{0,1:T(8,128)(2,1)S(1)}, u32[]{:S(2)}) copy-start(bf16[6912,192]{0,1:T(8,128)(2,1)S(1)} %fusion.1) | copy-start | bytes 7962628
  583.7 11.3 %collective-permute-start.6 = (bf16[192,192]{1,0:T(8,128)(2,1)S(1)}, bf16[192,192]{1,0:T(8,128)(2,1)}, u32[]{:S(2)}, u32[]{:S(2)}) collective-permute-start(bf16[192,192]{1,0:T(8,128)(2,1)S(1)} %get-tuple-element.48), channel_id=1, source_target_pairs={{0,4},{4,8},{8,12},{12,16},{16,20},{20,24},{24,28},{1,5},{5,9},{9,... | collective-permute-start | bytes 221192 | tf_op jit(solution)/shard_map/ppermute | solution.py:18
  587.7 43.4 %copy-start.46 = (f32[512]{0:T(512)S(1)}, f32[512]{0:T(512)}, u32[]{:S(2)}) copy-start(f32[512]{0:T(512)} %param.26) | copy-start | bytes 6148
  587.7 43.4 %copy-start.57 = (f32[192]{0:T(256)S(1)}, f32[192]{0:T(256)}, u32[]{:S(2)}) copy-start(f32[192]{0:T(256)} %copy-done.56) | copy-start | bytes 2308
  587.7 43.4 %copy-start.59 = (f32[192]{0:T(256)S(1)}, f32[192]{0:T(256)}, u32[]{:S(2)}) copy-start(f32[192]{0:T(256)} %copy-done.58) | copy-start | bytes 2308
  587.7 7.3 collective-permute-start.7
  597.9 72.4 %all-reduce.26.cloned.1.call-start = ((), (), s32[]{:S(2)}) async-start(), calls=%async_computation.9 | async-start | bytes 393216 | tf_op jit(solution)/shard_map/psum | solution.py:79
  638.4 31.9 %copy-start.48 = (f32[512]{0:T(512)S(1)}, f32[512]{0:T(512)}, u32[]{:S(2)}) copy-start(f32[512]{0:T(512)} %param.23) | copy-start | bytes 6148
  638.4 31.9 %copy-start.51 = (f32[192]{0:T(256)S(1)}, f32[192]{0:T(256)}, u32[]{:S(2)}) copy-start(f32[192]{0:T(256)} %copy-done.50) | copy-start | bytes 2308
  638.4 31.9 %copy-start.54 = (f32[192]{0:T(256)S(1)}, f32[192]{0:T(256)}, u32[]{:S(2)}) copy-start(f32[192]{0:T(256)} %copy-done.53) | copy-start | bytes 2308
  638.4 35.2 %copy-start.24 = (bf16[128,512]{1,0:T(8,128)(2,1)S(1)}, bf16[128,512]{1,0:T(8,128)(2,1)}, u32[]{:S(2)}) copy-start(bf16[128,512]{1,0:T(8,128)(2,1)} %param.22) | copy-start | bytes 393220
  638.5 166.2 %reduce-scatter.5.cloned.1.call-start = ((), (), s32[]{:S(2)}) async-start(), calls=%async_computation.10 | async-start | bytes 245760 | tf_op jit(solution)/shard_map/reduce_scatter | solution.py:314
  722.7 11.0 %copy-start.22 = (bf16[1216,128]{1,0:T(8,128)(2,1)S(1)}, bf16[1216,128]{1,0:T(8,128)(2,1)}, u32[]{:S(2)}) copy-start(bf16[1216,128]{1,0:T(8,128)(2,1)} %param.21) | copy-start | bytes 933892
  725.7 8.2 collective-permute-start.8
  729.7 6.3 collective-permute-start.9
  738.3 67.8 %reduce-scatter.7.cloned.1.call-start = ((), (), s32[]{:S(2)}) async-start(), calls=%async_computation.11 | async-start | bytes 4423680
  748.9 215.4 %all-reduce.28.cloned.1.call-start = ((), (), s32[]{:S(2)}) async-start(), calls=%async_computation.12 | async-start | bytes 8323072 | tf_op jit(solution)/shard_map/psum | solution.py:341
  749.5 15.5 %slice-start = ((s8[7077888]{0:T(1024)(128)(4,1)}), s8[4194304]{0:T(1024)(128)(4,1)S(1)}, s32[]{:S(2)}) async-start(s8[7077888]{0:T(1024)(128)(4,1)} %bitcast.43), calls=%async_computation.13 | async-start | bytes 8388608
  754.5 10.5 %slice-start.1 = ((s8[7077888]{0:T(1024)(128)(4,1)}), s8[2883584]{0:T(1024)(128)(4,1)S(1)}, s32[]{:S(2)}) async-start(s8[7077888]{0:T(1024)(128)(4,1)} %bitcast.43), calls=%async_computation.14 | async-start | bytes 5767168
  (40 other events, 183.8 us)
Sparse Core Ops, SparseCore 0:
  87.5 33.2 all-reduce.11
  126.2 31.7 all-reduce.13
  220.1 31.6 all-reduce.15
  256.8 31.7 all-reduce.17
  361.1 60.4 all-reduce.19
  449.7 60.5 all-reduce.21
  598.0 32.9 all-reduce.23
  638.5 31.7 all-reduce.25
  738.5 19.1 reduce-scatter.4
  760.0 40.4 reduce-scatter.6
  806.7 157.5 all-reduce.27
where the time goes:
time: 991 us; the launch traced here: 980 us
  waiting for transfers between devices  438 us (44%)
  local copies, waits for them, and re-layouts  206 us (21%)
  other arithmetic  178 us (18%)
  matrix products  90.2 us (9%)
  starting transfers between devices  31.2 us (3%)
  blocking collectives  20.8 us (2%)
  between operations  15.3 us (2%)
    psum x6, waiting for transfers between devices, model_sum(): return lax.psum(values.astype(jnp.bfloat16), 'mp').astype(jnp.float32)  189 us
    psum x1, waiting for transfers between devices, on_device(): lax.psum((msg_in_grad, g_msg_out, g_gain_a, g_ffn_in, g_ffn_out, g_gain_b...  150 us
    psum x2, waiting for transfers between devices, edge_total(): return lax.psum(values.astype(jnp.bfloat16), 'mp').astype(jnp.float32)  96.5 us
    scatter-add x2, other arithmetic, neighbour_back(): jax.ops.segment_sum(d_float, local_index, num_segments=3 * height)  73.2 us
    gather x4, local copies, waits for them, and re-layouts, neighbour_terms(): jnp.take(product(extended, other_weight), local_index, axis=0)  52.2 us
    dot_general x15, matrix products, product(): return jnp.dot(left_side, right_side, preferred_element_type=jnp.float32)  51.7 us
    add x7, local copies, waits for them, and re-layouts, neighbour_terms(): return (self_term[:, None, :] + other_term).reshape(count * degree, -1)  33.7 us
    mul x4, other arithmetic, smooth(): return jax.nn.gelu(values, approximate=False)  26.7 us
  transfers between devices with their start and end apart: 21, of which 10 were waited for; matrix products, arithmetic and copies ran while one was open for 15% of the time, Pallas kernels for 0%

commit v1 on v0

v1 whole, which is shorter than its diff:
```python
import functools
import math
from types import SimpleNamespace

import jax
import jax.numpy as jnp
from jax import lax
from jax.experimental import pallas as pl
from jax.experimental.pallas import tpu as pltpu
from jax.sharding import PartitionSpec as P

EPSILON = 1e-05
F32 = jnp.float32
BF16 = jnp.bfloat16
MESH = pl.DeviceIdType.MESH
ROOT_TWO_PI = 0.3989422804014327
SCALE = 0.3275911 * 0.7071067811865476
TAIL = (0.127414796, -0.142248368, 0.7107068705, -0.7265760135, 0.5307027145)
ANY = pl.BlockSpec(memory_space=pl.ANY)
VMEM = pl.BlockSpec(memory_space=pltpu.VMEM)


def dot(left, right):
    return jnp.dot(left, right, preferred_element_type=F32)


def dot_bt(left, right):
    return lax.dot_general(left, right, (((1,), (1,)), ((), ())), preferred_element_type=F32)


def dot_at(left, right):
    return lax.dot_general(left, right, (((0,), (0,)), ((), ())), preferred_element_type=F32)


def bell(v):
    t = 1.0 / (1.0 + SCALE * jnp.abs(v))
    fall = jnp.exp(-0.5 * (v * v))
    poly = TAIL[4]
    for c in (TAIL[3], TAIL[2], TAIL[1], TAIL[0]):
        poly = c + t * poly
    tail = t * poly * fall
    return jnp.where(v >= 0.0, 1.0 - tail, tail), fall


def norm_parts(values, width):
    scale = 1.0 / width
    centred = values - jnp.sum(values, axis=-1, keepdims=True) * scale
    inverse = lax.rsqrt(jnp.sum(centred * centred, axis=-1, keepdims=True) * scale + EPSILON)
    return centred * inverse, inverse


def norm_back(upstream, normed, inverse, gain, width):
    scale = 1.0 / width
    scaled = upstream * gain
    mean = jnp.sum(scaled, axis=-1, keepdims=True) * scale
    along = jnp.sum(scaled * normed, axis=-1, keepdims=True) * scale
    return inverse * (scaled - mean - normed * along)


def up(rows, step):
    return -(-rows // step) * step


class Net:
    def __init__(self, send, recv, local):
        self.send, self.recv, self.local = send, recv, local
        self.remote_count = 0
        self.local_count = 0

    def remote(self, src, dst, side="", **where):
        i = self.remote_count
        self.remote_count += 1
        return pltpu.make_async_remote_copy(
            src_ref=src,
            dst_ref=dst,
            send_sem=self.send.at[i],
            recv_sem=self.recv.at[i],
            device_id=where,
            device_id_type=MESH,
        )

    def reserve(self, count):
        i = self.remote_count
        self.remote_count += count
        return i

    def at(self, i, src, dst, **where):
        return pltpu.make_async_remote_copy(
            src_ref=src,
            dst_ref=dst,
            send_sem=self.send.at[i],
            recv_sem=self.recv.at[i],
            device_id=where,
            device_id_type=MESH,
        )

    def opened(self, i, src, dst, **where):
        return self.at(i, src, dst, **where)

    def copy(self, src, dst):
        i = self.local_count
        self.local_count += 1
        c = pltpu.make_async_copy(src, dst, self.local.at[i])
        c.start()
        return c


def kernel_body(S, in_names, out_names, scratch_names, *refs):
    names = in_names + out_names + scratch_names
    A = SimpleNamespace(**dict(zip(names, refs, strict=True)))
    net = Net(A.send, A.recv, A.local)
    RB, RQ, K, D, DE, HM, HE, FL = S.RB, S.RQ, S.K, S.D, S.DE, S.HM, S.HE, S.FL
    E = RQ * K
    W = 3 * RB
    EC = 6 * RQ
    res = lax.axis_index("res")
    mp = lax.axis_index("mp")
    has_l = res > 0
    has_r = res < S.n_res - 1
    pair = mp + 1 - 2 * (mp % 2)
    cross = (mp + 2) % 4
    third = (pair + 2) % 4

    def peer(d):
        return (mp + d) % 4

    def rows_at(start, size, step=16):
        return pl.ds(pl.multiple_of(start, step), size)

    def quarter(q, base=0):
        return rows_at(base + RQ * q, RQ)

    load_nodes = net.copy(A.nodes, A.nodes_v)
    load_nbr = net.copy(A.neighbours, A.nbr_v)
    load_mask = net.copy(A.edge_mask, A.mask_v)
    load_edges = net.copy(A.edges.at[quarter(mp)], A.e_v)
    own_msg_in = A.Wm.at[:, pl.ds(pl.multiple_of(mp * 128, 128), 128)]
    load_msg_in = net.copy(A.msg_in, own_msg_in)
    own_msg_out = A.Wo.at[rows_at(mp * 128, 128)]
    load_msg_out = net.copy(A.msg_out, own_msg_out)
    load_ffn_in = net.copy(A.ffn_in, A.fi_v)
    load_ffn_out = net.copy(A.ffn_out, A.fo_v)
    big, small = HE // 4 // 3 * 2, HE // 4 // 3

    def main_rows(ref):
        return lambda q: ref.at[rows_at(big * q, big)]

    def rest_rows(ref):
        return lambda q: ref.at[rows_at(4 * big + small * q, small)]

    first, rest = pl.ds(0, big), pl.ds(big, small)
    edge_parts = (
        (A.edge_in.at[first], main_rows(A.We)),
        (A.edge_out.at[first], main_rows(A.Eo)),
        (A.edge_in.at[rest], rest_rows(A.We)),
        (A.edge_out.at[rest], rest_rows(A.Eo)),
    )
    load_edge_weights = [net.copy(src, place(mp)) for src, place in edge_parts]
    load_node_cot = net.copy(A.node_cot.at[quarter(mp)], A.nc_v)
    load_edge_cot = net.copy(A.edge_cot.at[quarter(mp)], A.ec_v)

    barrier = pltpu.get_barrier_semaphore()

    def greet(**where):
        pl.semaphore_signal(barrier, inc=1, device_id=where, device_id_type=MESH)

    def across(s):
        return res + (1 << s) * (1 - 2 * ((res // (1 << s)) % 2))

    for d in (1, 2, 3):
        greet(mp=peer(d))
    for s in range(S.bits):
        greet(res=across(s))

    @pl.when(has_l)
    def _():
        greet(res=res - 1)

    @pl.when(has_r)
    def _():
        greet(res=res + 1)

    sides = (res + S.n_res - 1) // S.n_res + 1 - (res + 1) // S.n_res
    pl.semaphore_wait(barrier, 3 + S.bits + sides)

    class Spread:
        def __init__(self, src, place):
            own = place(mp)
            self.first = [net.remote(src, own, mp=pair), net.remote(src, own, mp=cross)]
            self.then = net.remote(place(cross), place(cross), mp=pair)

        def start(self):
            for c in self.first:
                c.start()

        def forward(self):
            self.first[1].wait_recv()
            self.then.start()

        def wait(self):
            self.first[0].wait_recv()
            self.then.wait_recv()

        def sent(self):
            for c in self.first:
                c.wait_send()
            self.then.wait_send()

    spread_msg_in = Spread(
        A.msg_in, lambda q: A.Wm.at[:, pl.ds(pl.multiple_of(q * 128, 128), 128)]
    )
    spread_msg_out = Spread(A.msg_out, lambda q: A.Wo.at[rows_at(q * 128, 128)])
    spread_edge = [Spread(src, place) for src, place in edge_parts]

    def clear_sides(win):
        @pl.when(jnp.logical_not(has_l))
        def _():
            win[0:RB] = jnp.zeros((RB, D), BF16)

        @pl.when(jnp.logical_not(has_r))
        def _():
            win[2 * RB : 3 * RB] = jnp.zeros((RB, D), BF16)

    half = RB // 2

    class Halo:
        def __init__(self, win):
            h = mp % 2
            own = win.at[rows_at(RB + half * h, half)]
            left = win.at[rows_at(half * h, half)]
            right = win.at[rows_at(2 * RB + half * h, half)]
            self.to_l = net.remote(own, right, side="l", res=res - 1)
            self.to_r = net.remote(own, left, side="r", res=res + 1)
            self.on_l = net.remote(left, left, mp=pair)
            self.on_r = net.remote(right, right, mp=pair)

        def start(self):
            pl.when(has_l)(self.to_l.start)
            pl.when(has_r)(self.to_r.start)

        def forward(self):
            @pl.when(has_l)
            def _():
                self.to_r.wait_recv()
                self.on_l.start()

            @pl.when(has_r)
            def _():
                self.to_l.wait_recv()
                self.on_r.start()

        def wait(self):
            pl.when(has_l)(self.on_l.wait_recv)
            pl.when(has_r)(self.on_r.wait_recv)

        def sent(self):
            @pl.when(has_l)
            def _():
                self.to_l.wait_send()
                self.on_l.wait_send()

            @pl.when(has_r)
            def _():
                self.to_r.wait_send()
                self.on_r.wait_send()

    class Window:
        def __init__(self, win):
            own = win.at[quarter(mp, RB)]
            left = win.at[quarter(mp)]
            right = win.at[quarter(mp, 2 * RB)]
            self.to_l = net.remote(own, right, side="l", res=res - 1)
            self.to_r = net.remote(own, left, side="r", res=res + 1)
            self.mine = [net.remote(own, own, mp=peer(d)) for d in (1, 2, 3)]
            self.on_l = [net.remote(left, left, mp=peer(d)) for d in (1, 2, 3)]
            self.on_r = [net.remote(right, right, mp=peer(d)) for d in (1, 2, 3)]

        def start(self):
            pl.when(has_l)(self.to_l.start)
            pl.when(has_r)(self.to_r.start)
            for c in self.mine:
                c.start()

        def forward(self):
            @pl.when(has_l)
            def _():
                self.to_r.wait_recv()
                for c in self.on_l:
                    c.start()

            @pl.when(has_r)
            def _():
                self.to_l.wait_recv()
                for c in self.on_r:
                    c.start()

        def wait_own(self):
            for c in self.mine:
                c.wait_recv()

        def wait(self):
            @pl.when(has_l)
            def _():
                for c in self.on_l:
                    c.wait_recv()

            @pl.when(has_r)
            def _():
                for c in self.on_r:
                    c.wait_recv()

        def sent(self):
            for c in self.mine:
                c.wait_send()

            @pl.when(has_l)
            def _():
                self.to_l.wait_send()
                for c in self.on_l:
                    c.wait_send()

            @pl.when(has_r)
            def _():
                self.to_r.wait_send()
                for c in self.on_r:
                    c.wait_send()

    def gather_rows(buf):
        own = buf.at[quarter(mp)]
        copies = [net.remote(own, own, mp=peer(d)) for d in (1, 2, 3)]
        for c in copies:
            c.start()
        return copies

    def scatter_sum_start(buf, into):
        copies = [
            net.remote(buf.at[quarter(peer(d))], into.at[d - 1], mp=peer(d)) for d in (1, 2, 3)
        ]
        for c in copies:
            c.start()
        return copies

    def landed(copies):
        for c in copies:
            c.wait_recv()

    late = []

    def return_rows(product, send, recv, side_send, side_recv, fill, between):
        for blk in range(3):
            part = product(blk)
            for q in range(4):
                send[q, blk] = part[RQ * q : RQ * q + RQ].astype(BF16)
        copies = [net.remote(send.at[peer(d)], recv.at[d - 1], mp=peer(d)) for d in (1, 2, 3)]
        for c in copies:
            c.start()
        fill()
        landed(copies)
        late.extend(copies)

        def total(blk):
            out = send[mp, blk].astype(F32)
            for d in range(3):
                out = out + recv[d, blk].astype(F32)
            return out

        side_send[0] = total(0).astype(BF16)
        side_send[1] = total(2).astype(BF16)
        to_l = net.remote(side_send.at[0], side_recv.at[1], side="l", res=res - 1)
        to_r = net.remote(side_send.at[1], side_recv.at[0], side="r", res=res + 1)
        pl.when(has_l)(to_l.start)
        pl.when(has_r)(to_r.start)
        mid = total(1)
        between()
        pl.when(has_l)(to_r.wait_recv)
        pl.when(has_r)(to_l.wait_recv)
        pl.when(has_l)(to_l.wait_send)
        pl.when(has_r)(to_r.wait_send)
        return mid + side_recv[0].astype(F32) + side_recv[1].astype(F32)

    spread_msg_in.start()
    spread_msg_out.start()
    load_nodes.wait()

    @pl.loop(0, RB // 16)
    def _(i):
        A.win1[rows_at(RB + 16 * i, 16)] = A.nodes_v[rows_at(16 * i, 16)].astype(BF16)

    halo = Halo(A.win1)
    halo.start()
    for win in (A.win1, A.win2, A.win3):
        clear_sides(win)
    for ref in (A.back_side_a, A.back_side_b):
        ref[...] = jnp.zeros_like(ref)

    load_nbr.wait()
    load_mask.wait()
    load_edges.wait()
    stack = jnp.concatenate(
        [A.nbr_v[...].astype(F32), A.mask_v[...].astype(F32), jnp.zeros((128 - 2 * K, RB), F32)],
        axis=0,
    )
    stack = jnp.concatenate([stack, jnp.zeros((128, 256 - RB), F32)], axis=1)
    A.columns[...] = jnp.transpose(stack)[0:RB]
    columns = A.columns[rows_at(RQ * mp, RQ)]
    local = columns[:, 0:K].astype(jnp.int32) - (res - 1) * RB + DE
    live = columns[:, K : 2 * K]
    mean_weight = live / jnp.maximum(jnp.sum(live, axis=1, keepdims=True), 1.0)
    lane256 = lax.broadcasted_iota(jnp.int32, (RQ, 256), 1)
    lane512 = lax.broadcasted_iota(jnp.int32, (RQ, 512), 1) + 256
    is_edge = lane256 < DE

    def pair_load(buf, base):
        even = buf[:, pl.ds(base, 256)]
        odd = pltpu.roll(buf[:, pl.ds(base + 128, 256)], 192, 1)
        return jnp.where(is_edge, even, 0.0), jnp.where(is_edge, odd, 0.0)

    def pair_store(buf, base, even, odd, sub=slice(None)):
        back = pltpu.roll(odd, 64, 1)
        buf[sub, pl.ds(base, 128)] = even[:, :128].astype(buf.dtype)
        buf[sub, pl.ds(base + 128, 128)] = (even[:, 128:] + back[:, :128]).astype(buf.dtype)
        buf[sub, pl.ds(base + 256, 128)] = back[:, 128:].astype(buf.dtype)

    for j in range(K // 2):
        both = pair_load(A.e_v, 384 * j)
        for p in range(2):
            k = 2 * j + p
            column = local[:, k : k + 1]
            hot = jnp.where(column == lane256, 1.0, 0.0)
            A.XE[RQ * k : RQ * k + RQ] = jnp.where(is_edge, both[p], hot).astype(BF16)
            A.XO[RQ * k : RQ * k + RQ] = jnp.where(column == lane512, 1.0, 0.0).astype(BF16)
            A.WB[RQ * k : RQ * k + RQ] = jnp.broadcast_to(mean_weight[:, k : k + 1], (RQ, 128))

    halo.forward()

    full = E // 128

    @pl.loop(0, full)
    def _(c):
        at = pl.ds(pl.multiple_of(128 * c, 128), 128)
        A.XT[0:256, at] = A.XE[at].T
        A.XT[256:768, at] = A.XO[at].T

    if E % 128:
        at = slice(full * 128, E)
        A.XT[0:256, at] = A.XE[at].T
        A.XT[256:768, at] = A.XO[at].T

    spread_msg_in.forward()
    spread_msg_out.forward()
    halo.wait()

    gain_a = A.gain_a[...]
    gain_b = A.gain_b[...]
    load_msg_in.wait()
    load_msg_out.wait()

    def node_table(win):
        for blk in (1, 0, 2):
            part = dot(win[RB * blk : RB * blk + RB], A.Wm[D : 2 * D])
            A.T[DE + RB * blk : DE + RB * blk + RB] = part.astype(BF16)

    def message_mean(win, keep):
        A.selfs[...] = dot(win[quarter(mp, RB)], A.Wm[0:D])
        A.total[...] = jnp.zeros((RQ, HM), F32)

        @pl.loop(0, E // EC)
        def _(c):
            rows = rows_at(EC * c, EC)
            left = jnp.concatenate([A.XE[rows], A.XO[rows]], axis=1)
            A.base[:, 0:HM] = dot(left, A.T[...])

            @pl.loop(0, RQ // 16)
            def _(sub):
                own = rows_at(16 * sub, 16)
                mine = A.selfs[own]
                total = A.total[own]
                for k in range(6):
                    v = A.base[rows_at(RQ * k + 16 * sub, 16), 0:HM] + mine
                    at = rows_at(EC * c + RQ * k + 16 * sub, 16)
                    w = jnp.concatenate([A.WB[at]] * (HM // 128), axis=1)
                    phi, fall = bell(v)
                    if keep:
                        A.slope[at] = (w * (phi + v * fall * ROOT_TWO_PI)).astype(BF16)
                    total = total + w * (v * phi)
                A.total[own] = total

        A.avg[...] = A.total[...].astype(BF16)

    def node_tail(states, ug, part_b, part_r, keep):
        normed_a, inverse_a = norm_parts(states + dot(A.avg[...], A.Wo[...]), D)
        middle = normed_a * gain_a
        ug[quarter(mp)] = middle.astype(BF16)
        moved = gather_rows(ug)
        landed(moved)
        late.extend(moved)
        A.hid[...] = dot(ug[...], A.fi_v[...])

        @pl.loop(0, RB // 16)
        def _(i):
            rows = rows_at(16 * i, 16)
            v = A.hid[rows]
            phi, fall = bell(v)
            A.smooth[rows] = (v * phi).astype(BF16)
            if keep:
                A.hslope[rows] = phi + v * fall * ROOT_TWO_PI

        A.part[...] = dot(A.smooth[...], A.fo_v[...])
        part_b[...] = A.part[...].astype(BF16)
        moved = scatter_sum_start(part_b, part_r)
        total = middle + A.part[quarter(mp)]
        landed(moved)
        late.extend(moved)
        for d in range(3):
            total = total + part_r[d].astype(F32)
        normed_b, inverse_b = norm_parts(total, D)
        if keep:
            A.normed_a[...] = normed_a
            A.inverse_a[...] = jnp.broadcast_to(inverse_a, (RQ, 128))
            A.normed_b[...] = normed_b
            A.inverse_b[...] = jnp.broadcast_to(inverse_b, (RQ, 128))
        return normed_b * gain_b

    spread_msg_in.wait()
    spread_edge[0].start()
    spread_edge[1].start()
    A.T[0:DE] = A.Wm[2 * D : 2 * D + DE]
    node_table(A.win1)
    message_mean(A.win1, False)
    spread_msg_out.wait()
    load_ffn_in.wait()
    load_ffn_out.wait()
    own_nodes = A.nodes_v[quarter(mp)]
    predicted = node_tail(own_nodes, A.ug1, A.pb1, A.pr1, False)
    A.mixed[...] = 0.5 * (own_nodes + predicted)
    A.win2[quarter(mp, RB)] = A.mixed[...].astype(BF16)
    window2 = Window(A.win2)
    window2.start()
    window2.forward()
    window2.wait_own()
    window2.wait()
    spread_edge[2].start()
    spread_edge[3].start()
    spread_edge[0].forward()
    spread_edge[1].forward()
    node_table(A.win2)
    message_mean(A.win2, True)
    spread_edge[2].forward()
    spread_edge[3].forward()
    settled = node_tail(A.mixed[...], A.ug2, A.pb2, A.pr2, True)
    A.win3[quarter(mp, RB)] = settled.astype(BF16)
    window3 = Window(A.win3)
    window3.start()
    window3.forward()

    for c in (*spread_edge, *load_edge_weights):
        c.wait()
    A.Eop[...] = jnp.concatenate([A.Eo[...], jnp.zeros((HE, 64), BF16)], axis=1)
    A.Te[0:DE] = A.We[:, 2 * D : 2 * D + DE].T
    window3.wait_own()
    window3.wait()
    store = [net.copy(A.win3.at[RB : 2 * RB], A.out_nodes)]

    for blk in (1, 0, 2):
        part = dot_bt(A.win3[RB * blk : RB * blk + RB], A.We[:, D : 2 * D])
        A.Te[DE + RB * blk : DE + RB * blk + RB] = part.astype(BF16)
    A.selfe[...] = dot_bt(A.win3[quarter(mp, RB)], A.We[:, 0:D])
    A.dself[...] = jnp.zeros((RQ, HE), F32)
    load_edge_cot.wait()
    gain_c = jnp.concatenate([A.gain_c[...], jnp.zeros((1, 256 - DE), F32)], axis=1)

    def norm_parts_e(values):
        scale = 1.0 / DE
        mean = jnp.sum(values, axis=-1, keepdims=True) * scale
        centred = jnp.where(is_edge, values - mean, 0.0)
        inverse = lax.rsqrt(jnp.sum(centred * centred, axis=-1, keepdims=True) * scale + EPSILON)
        return centred * inverse, inverse

    chunks = E // EC
    stream = net.reserve(3 * chunks)

    def new_part(q, c):
        return A.new_edges.at[quarter(q), pl.ds(pl.multiple_of(6 * DE * c, 128), 6 * DE)]

    def stream_copies(make, c):
        return (
            make(stream + c, new_part(mp, c), new_part(mp, c), mp=pair),
            make(stream + chunks + c, new_part(mp, c), new_part(mp, c), mp=cross),
            make(stream + 2 * chunks + c, new_part(cross, c), new_part(cross, c), mp=pair),
        )

    def edge_chunk(c, gain_total):
        rows = rows_at(EC * c, EC)
        A.base[...] = dot(A.XO[rows], A.Te[256:768])
        A.pre2[...] = dot(A.XE[rows], A.Te[0:256])

        @pl.loop(0, EC // 16)
        def _(b):
            at = rows_at(16 * b, 16)
            base = A.base[at] + A.selfe[rows_at(16 * (b % (RQ // 16)), 16)]
            A.base[at] = base
            v = base + A.pre2[at]
            phi, _ = bell(v)
            A.G[at] = (v * phi).astype(BF16)

        A.upd[...] = dot(A.G[...], A.Eop[...])
        for j in range(3):
            both = pair_load(A.e_v, pl.multiple_of(1152 * c + 384 * j, 128))
            for p in range(2):
                k = 2 * j + p
                mine = slice(RQ * k, RQ * k + RQ)
                at = rows_at(EC * c + RQ * k, RQ)
                normed, _ = norm_parts_e(both[p] + A.upd[mine])
                mixed = 0.5 * (both[p] + normed * gain_c)
                A.emix[mine] = mixed
                A.XM[at] = jnp.where(is_edge, mixed, A.XE[at].astype(F32)).astype(BF16)

        A.pre2[...] = dot(A.XM[rows], A.Te[0:256])

        @pl.loop(0, EC // 16)
        def _(b):
            at = rows_at(16 * b, 16)
            v = A.base[at] + A.pre2[at]
            phi, fall = bell(v)
            A.G2[rows_at(EC * c + 16 * b, 16)] = (v * phi).astype(BF16)
            A.base[at] = phi + v * fall * ROOT_TWO_PI

        A.upd[...] = dot(A.G2[rows], A.Eop[...])
        for j in range(3):
            lanes = pl.multiple_of(1152 * c + 384 * j, 128)
            cots = pair_load(A.ec_v, lanes)
            news = []
            for p in range(2):
                k = 2 * j + p
                mine = slice(RQ * k, RQ * k + RQ)
                normed, inverse = norm_parts_e(A.emix[mine] + A.upd[mine])
                news.append(normed * gain_c)
                gain_total = gain_total + jnp.sum(
                    (cots[p] * normed).reshape(RQ // 8, 8, 256), axis=0
                )
                d_sum = jnp.where(is_edge, norm_back(cots[p], normed, inverse, gain_c, DE), 0.0)
                A.emix[mine] = d_sum
                A.DO[rows_at(EC * c + RQ * k, RQ)] = d_sum.astype(BF16)
            pair_store(A.new_edges, lanes, news[0], news[1], quarter(mp))

        to_pair, to_cross, _ = stream_copies(net.at, c)
        to_cross.start()
        to_pair.start()

        @pl.when(c > 0)
        def _():
            _, arrived, on = stream_copies(net.at, c - 1)
            arrived.wait_recv()
            on.start()


        A.pre2[...] = dot_bt(A.DO[rows], A.Eop[...])

        @pl.loop(0, EC // 16)
        def _(b):
            at = rows_at(16 * b, 16)
            own = rows_at(16 * (b % (RQ // 16)), 16)
            d = (A.pre2[at] * A.base[at]).astype(BF16)
            A.DP2[rows_at(EC * c + 16 * b, 16)] = d
            A.dself[own] = A.dself[own] + d.astype(F32)

        A.EG[rows] = 0.5 * (A.emix[...] + dot_bt(A.DP2[rows], A.Te[0:256]))
        return gain_total

    gain_total = lax.fori_loop(0, E // EC, edge_chunk, jnp.zeros((8, 256), F32))
    A.gains[...] = jnp.zeros_like(A.gains)
    A.gains[2:3, 0:256] = jnp.sum(gain_total, axis=0, keepdims=True)

    streams = [stream_copies(net.opened, c) for c in range(chunks - 1)]
    last_pair, last_cross, _ = stream_copies(net.opened, chunks - 1)
    on_last = net.remote(new_part(cross, chunks - 1), new_part(cross, chunks - 1), mp=pair)

    A.dself_low[...] = A.dself[...].astype(BF16)
    for blk in range(3):
        at = slice(RB * blk, RB * blk + RB)
        A.dq[at] = dot(A.XT[DE + RB * blk : DE + RB * blk + RB], A.DP2[...]).astype(BF16)

    load_node_cot.wait()

    def emit_edge(tile, value):
        for q in range(4):
            at = DE * tile
            A.ge[q, at : at + big] = value[big * q : big * q + big].astype(BF16)
            more = 4 * big + small * q
            A.ge[q, at + big : at + DE] = value[more : more + small].astype(BF16)

    def emit_msg(row, value):
        n = value.shape[0]
        for q in range(4):
            A.gm[q, row : row + n] = value[:, 128 * q : 128 * q + 128].astype(BF16)

    def edge_weight_gradients():
        by_in = dot_at(A.XM[...], A.DP2[...])
        by_out = dot_at(A.DO[...], A.G2[...])
        emit_edge(8, jnp.transpose(by_in[0:128]))
        emit_edge(10, jnp.transpose(by_out[0:128]))
        emit_edge(
            9, jnp.transpose(jnp.concatenate([by_in[128:DE], by_out[128:DE]], axis=0))
        )
        own = A.win3[quarter(mp, RB)]
        for t in range(4):
            at = slice(128 * t, 128 * t + 128)
            emit_edge(t, jnp.transpose(dot_at(own[:, at], A.dself_low[...])))
            emit_edge(4 + t, jnp.transpose(dot_at(A.win3[:, at], A.dq[...])))
        pump(sum_edge)

    def message_weight_gradients():
        own = A.win2[quarter(mp, RB)]
        for t in range(4):
            at = slice(128 * t, 128 * t + 128)
            emit_msg(128 * t, dot_at(own[:, at], A.dmsg_low[...]))
            emit_msg(D + 128 * t, dot_at(A.win2[:, at], A.dq1[...]))
            value = dot_at(A.avg[:, at], A.dg1[...])
            for u in range(4):
                row = 2 * D + DE + 128 * u
                A.gm[t, row : row + 128] = value[:, 128 * u : 128 * u + 128].astype(BF16)
        emit_msg(2 * D, dot(A.XT[0:DE], A.DP[...]))

    for ref, used in ((A.ge, 11 * DE), (A.gm, 3 * D + DE)):
        if ref.shape[1] > used:
            for q in range(4):
                ref[q, used:] = jnp.zeros((ref.shape[1] - used, 128), BF16)

    def reduce_mp(g, got, cuts):
        rows = g.shape[1]
        a1 = net.remote(g.at[pair], got.at[0], mp=pair)
        a2 = net.remote(g.at[third], got.at[1], mp=pair)
        a2.start()
        a1.start()
        yield
        a2.wait_recv()

        @pl.loop(0, rows // 32)
        def _(i):
            at = rows_at(32 * i, 32)
            got[1, at] = (g[cross, at].astype(F32) + got[1, at].astype(F32)).astype(BF16)

        step = rows // cuts
        pieces = []
        for i in range(cuts):
            at = pl.ds(step * i, step)
            b = net.remote(got.at[1, at], got.at[2, at], mp=cross)
            b.start()
            pieces.append(b)
            yield
        for c in (a1, *pieces):
            c.wait_recv()

        @pl.loop(0, rows // 32)
        def _(i):
            at = rows_at(32 * i, 32)
            total = g[mp, at].astype(F32) + got[0, at].astype(F32) + got[2, at].astype(F32)
            got[0, at] = total.astype(BF16)

        for c in (a1, a2, *pieces):
            c.wait_send()

    def reduce_res(work, got, out, result, order):
        size = work.shape[0]
        low = 0
        used = 0
        for s in order:
            bit = (res // (1 << s)) % 2
            size = size // 2
            keep = low + bit * size
            give = low + (1 - bit) * size
            c = net.remote(
                work.at[rows_at(give, size, S.grain)], got.at[pl.ds(used, size)], res=across(s)
            )
            c.start()
            yield
            c.wait()
            into = out if s == order[-1] else work

            @pl.loop(0, size // S.grain)
            def _(i, keep=keep, used=used, into=into):
                at = rows_at(keep + S.grain * i, S.grain, S.grain)
                there = rows_at(used + S.grain * i, S.grain, S.grain)
                into[at] = (work[at].astype(F32) + got[there].astype(F32)).astype(BF16)

            used += size
            low = keep
        for s in reversed(order):
            bit = (res // (1 << s)) % 2
            here = out.at[rows_at(low, size, S.grain)]
            c = net.remote(here, here, res=across(s))
            c.start()
            yield
            c.wait()
            low = low - bit * size
            size = 2 * size
        store.append(net.copy(out, result))

    def reduce_gains():
        copies = [net.remote(A.gains, A.gains_r.at[d - 1], mp=peer(d)) for d in (1, 2, 3)]
        for c in copies:
            c.start()
        yield
        for c in copies:
            c.wait()
        A.gains_t[0] = A.gains[...] + A.gains_r[0] + A.gains_r[1] + A.gains_r[2]
        for s in range(S.bits):
            c = net.remote(A.gains_t.at[s], A.gains_r.at[3 + s], res=across(s))
            c.start()
            yield
            c.wait()
            A.gains_t[s + 1] = A.gains_t[s] + A.gains_r[3 + s]
        store.append(net.copy(A.gains_t.at[S.bits], A.out_gains))

    def chain(*parts):
        for part in parts:
            yield from part

    def pump(*sums):
        for g in sums:
            next(g, None)

    order = list(range(S.bits))
    sum_edge = chain(
        reduce_mp(A.ge, A.ge_r, 2), reduce_res(A.ge_r.at[0], A.sum_er, A.sum_e, A.pack_e, order)
    )
    sum_in = reduce_res(A.grad_i, A.sum_ir, A.sum_i, A.pack_i, order)
    sum_out = reduce_res(A.grad_o, A.sum_or, A.sum_o, A.pack_o, order)
    sum_msg = chain(
        reduce_mp(A.gm, A.gm_r, 1), reduce_res(A.gm_r.at[0], A.sum_mr, A.sum_m, A.pack_m, order)
    )
    sum_gains = reduce_gains()

    def between_a():
        last_cross.wait_recv()
        on_last.start()
        pump(sum_edge)

    d_settled = A.nc_v[...] + dot(A.dself_low[...], A.We[:, 0:D])
    d_settled = d_settled + return_rows(
        lambda blk: dot(A.dq[RB * blk : RB * blk + RB], A.We[:, D : 2 * D]),
        A.back_send_a,
        A.back_recv_a,
        A.back_side_send_a,
        A.back_side_a,
        edge_weight_gradients,
        between_a,
    )

    normed_b = A.normed_b[...]
    d_sum_b = norm_back(d_settled, normed_b, A.inverse_b[:, 0:1], gain_b, D)
    A.gains[1:2] = jnp.sum(d_settled * normed_b, axis=0, keepdims=True)
    A.dF[quarter(mp)] = d_sum_b.astype(BF16)
    moved = gather_rows(A.dF)
    landed(moved)
    late.extend(moved)
    A.hid[...] = dot_bt(A.dF[...], A.fo_v[...])

    @pl.loop(0, RB // 16)
    def _(i):
        rows = rows_at(16 * i, 16)
        A.dT[rows] = (A.hid[rows] * A.hslope[rows]).astype(BF16)

    A.part[...] = dot_bt(A.dT[...], A.fi_v[...])
    A.pb3[...] = A.part[...].astype(BF16)
    moved = scatter_sum_start(A.pb3, A.pr3)
    pump(sum_edge)
    A.grad_i[...] = dot_at(A.ug2[...], A.dT[...]).astype(BF16)
    pump(sum_in)
    A.grad_o[...] = dot_at(A.smooth[...], A.dF[...]).astype(BF16)
    pump(sum_out)
    d_middle = d_sum_b + A.part[quarter(mp)]
    landed(moved)
    late.extend(moved)
    for d in range(3):
        d_middle = d_middle + A.pr3[d].astype(F32)
    normed_a = A.normed_a[...]
    d_sum_a = norm_back(d_middle, normed_a, A.inverse_a[:, 0:1], gain_a, D)
    A.gains[0:1] = jnp.sum(d_middle * normed_a, axis=0, keepdims=True)
    pump(sum_gains)
    A.dsa[...] = d_sum_a
    A.dg1[...] = d_sum_a.astype(BF16)
    A.davg[...] = dot_bt(A.dg1[...], A.Wo[...])

    for sub in range(RQ // 16):
        mine = A.davg[16 * sub : 16 * sub + 16]

        def back_step(k, total, sub=sub, mine=mine):
            rows = rows_at(RQ * k + 16 * sub, 16)
            d = (mine * A.slope[rows].astype(F32)).astype(BF16)
            A.DP[rows] = d
            return total + d.astype(F32)

        total = lax.fori_loop(0, K, back_step, jnp.zeros((16, HM), F32))
        A.dmsg_low[16 * sub : 16 * sub + 16] = total.astype(BF16)

    for blk in range(3):
        at = slice(RB * blk, RB * blk + RB)
        A.dq1[at] = dot(A.XT[DE + RB * blk : DE + RB * blk + RB], A.DP[...]).astype(BF16)

    message_weight_gradients()
    pump(sum_msg, sum_edge, sum_in, sum_out, sum_gains)

    def edge_gradient():
        @pl.loop(0, E // EC)
        def _(c):
            rows = rows_at(EC * c, EC)
            A.EG[rows] = A.EG[rows] + dot_bt(A.DP[rows], A.T[0:256])
            for j in range(3):
                lanes = pl.multiple_of(1152 * c + 384 * j, 128)
                ends = [
                    jnp.where(is_edge, A.EG[rows_at(EC * c + RQ * (2 * j + p), RQ)], 0.0)
                    for p in range(2)
                ]
                pair_store(A.ec_v, lanes, ends[0], ends[1])

        store.append(net.copy(A.ec_v, A.out_edge_grad))
        for a, b, c in streams:
            a.wait()
            b.wait_send()
            c.wait()
        last_pair.wait()
        last_cross.wait_send()
        on_last.wait()
        store.append(net.copy(A.new_edges, A.out_edges))

    def fill_b():
        pump(sum_msg)
        edge_gradient()

    back = return_rows(
        lambda blk: dot_bt(A.dq1[RB * blk : RB * blk + RB], A.Wm[D : 2 * D]),
        A.back_send_b,
        A.back_recv_b,
        A.back_side_send_b,
        A.back_side_b,
        fill_b,
        lambda: pump(sum_in, sum_out, sum_edge, sum_msg, sum_gains),
    )
    A.node_grad_v[...] = 0.5 * (A.dsa[...] + dot_bt(A.dmsg_low[...], A.Wm[0:D]) + back)
    store.append(net.copy(A.node_grad_v, A.out_node_grad))

    work = [sum_in, sum_out, sum_edge, sum_msg, sum_gains]
    while work:
        for g in list(work):
            try:
                next(g)
            except StopIteration:
                work.remove(g)
    for c in store:
        c.wait()
    for s in (spread_msg_in, spread_msg_out, *spread_edge, halo, window2, window3):
        s.sent()
    for c in late:
        c.wait_send()
    assert net.remote_count <= S.remote and net.local_count <= S.local


def build(S):
    E = S.RQ * S.K
    W = 3 * S.RB
    EC = 6 * S.RQ
    grain = S.grain * S.n_res
    rows_e = up(11 * S.DE, grain)
    rows_m = up(3 * S.D + S.DE, grain)
    in_names = ["nodes", "edges", "neighbours", "edge_mask", "msg_in", "msg_out", "gain_a"]
    in_names += ["ffn_in", "ffn_out", "gain_b", "edge_in", "edge_out", "gain_c"]
    in_names += ["node_cot", "edge_cot"]
    outs = dict(
        out_nodes=((S.RB, S.D), BF16),
        out_edges=((S.RB, S.K * S.DE), BF16),
        out_node_grad=((S.RQ, S.D), F32),
        out_edge_grad=((S.RQ, S.K * S.DE), F32),
        pack_e=((rows_e, 128), BF16),
        pack_i=((S.D, S.FL), BF16),
        pack_o=((S.FL, S.D), BF16),
        pack_m=((rows_m, 128), BF16),
        out_gains=((8, S.D), F32),
    )
    scratch = dict(
        nodes_v=((S.RB, S.D), F32),
        nbr_v=((S.K, S.RB), jnp.int32),
        mask_v=((S.K, S.RB), jnp.int32),
        columns=((S.RB, 128), F32),
        new_edges=((S.RB, S.K * S.DE), BF16),
        node_grad_v=((S.RQ, S.D), F32),
        e_v=((S.RQ, S.K * S.DE), F32),
        ec_v=((S.RQ, S.K * S.DE), F32),
        nc_v=((S.RQ, S.D), F32),
        Wm=((2 * S.D + S.DE, S.HM), BF16),
        Wo=((S.HM, S.D), BF16),
        fi_v=((S.D, S.FL), BF16),
        fo_v=((S.FL, S.D), BF16),
        We=((S.HE, 2 * S.D + S.DE), BF16),
        Eo=((S.HE, S.DE), BF16),
        Eop=((S.HE, 256), BF16),
        win1=((W, S.D), BF16),
        win2=((W, S.D), BF16),
        win3=((W, S.D), BF16),
        XE=((E, 256), BF16),
        XM=((E, 256), BF16),
        XO=((E, 512), BF16),
        XT=((768, E), BF16),
        WB=((E, 128), F32),
        T=((768, S.HM), BF16),
        Te=((768, S.HE), BF16),
        selfs=((S.RQ, S.HM), F32),
        selfe=((S.RQ, S.HE), F32),
        total=((S.RQ, S.HM), F32),
        slope=((E, S.HM), BF16),
        avg=((S.RQ, S.HM), BF16),
        ug1=((S.RB, S.D), BF16),
        ug2=((S.RB, S.D), BF16),
        hid=((S.RB, S.FL), F32),
        smooth=((S.RB, S.FL), BF16),
        hslope=((S.RB, S.FL), F32),
        part=((S.RB, S.D), F32),
        pb1=((S.RB, S.D), BF16),
        pb2=((S.RB, S.D), BF16),
        pb3=((S.RB, S.D), BF16),
        pr1=((3, S.RQ, S.D), BF16),
        pr2=((3, S.RQ, S.D), BF16),
        pr3=((3, S.RQ, S.D), BF16),
        normed_a=((S.RQ, S.D), F32),
        normed_b=((S.RQ, S.D), F32),
        inverse_a=((S.RQ, 128), F32),
        inverse_b=((S.RQ, 128), F32),
        mixed=((S.RQ, S.D), F32),
        base=((EC, S.HE), F32),
        pre2=((EC, S.HE), F32),
        G=((EC, S.HE), BF16),
        upd=((EC, 256), F32),
        emix=((EC, 256), F32),
        G2=((E, S.HE), BF16),
        DO=((E, 256), BF16),
        DP2=((E, S.HE), BF16),
        EG=((E, 256), F32),
        dself=((S.RQ, S.HE), F32),
        dself_low=((S.RQ, S.HE), BF16),
        dq=((W, S.HE), BF16),
        gains=((8, S.D), F32),
        gains_r=((3 + S.bits, 8, S.D), F32),
        gains_t=((1 + S.bits, 8, S.D), F32),
        back_send_a=((4, 3, S.RQ, S.D), BF16),
        back_recv_a=((3, 3, S.RQ, S.D), BF16),
        back_side_send_a=((2, S.RQ, S.D), BF16),
        back_side_a=((2, S.RQ, S.D), BF16),
        back_send_b=((4, 3, S.RQ, S.D), BF16),
        back_recv_b=((3, 3, S.RQ, S.D), BF16),
        back_side_send_b=((2, S.RQ, S.D), BF16),
        back_side_b=((2, S.RQ, S.D), BF16),
        dF=((S.RB, S.D), BF16),
        dT=((S.RB, S.FL), BF16),
        dsa=((S.RQ, S.D), F32),
        dg1=((S.RQ, S.D), BF16),
        davg=((S.RQ, S.HM), F32),
        DP=((E, S.HM), BF16),
        dmsg_low=((S.RQ, S.HM), BF16),
        dq1=((W, S.HM), BF16),
        ge=((4, rows_e, 128), BF16),
        ge_r=((3, rows_e, 128), BF16),
        sum_er=((rows_e, 128), BF16),
        sum_e=((rows_e, 128), BF16),
        grad_i=((S.D, S.FL), BF16),
        sum_ir=((S.D, S.FL), BF16),
        sum_i=((S.D, S.FL), BF16),
        grad_o=((S.FL, S.D), BF16),
        sum_or=((S.FL, S.D), BF16),
        sum_o=((S.FL, S.D), BF16),
        gm=((4, rows_m, 128), BF16),
        gm_r=((3, rows_m, 128), BF16),
        sum_mr=((rows_m, 128), BF16),
        sum_m=((rows_m, 128), BF16),
    )
    names = list(scratch) + ["send", "recv", "local"]
    shapes = [pltpu.VMEM(*v) for v in scratch.values()] + [
        pltpu.SemaphoreType.DMA((S.remote,)),
        pltpu.SemaphoreType.DMA((S.remote,)),
        pltpu.SemaphoreType.DMA((S.local,)),
    ]
    body = functools.partial(kernel_body, S, in_names, list(outs), names)
    body.__name__ = "layer"
    gains = ("gain_a", "gain_b", "gain_c")
    return pl.pallas_call(
        body,
        name="layer",
        out_shape=[jax.ShapeDtypeStruct(*v) for v in outs.values()],
        in_specs=[VMEM if n in gains else ANY for n in in_names],
        out_specs=[ANY] * len(outs),
        scratch_shapes=shapes,
        compiler_params=pltpu.CompilerParams(
            collective_id=0, has_side_effects=True, vmem_limit_bytes=62 * 1024 * 1024
        ),
    )


def unpack_body(S, names, *refs):
    A = SimpleNamespace(**dict(zip(names, refs, strict=True)))
    D, DE, RB = S.D, S.DE, S.RB
    count = [0]

    def copy(src, dst):
        c = pltpu.make_async_copy(src, dst, A.sems.at[count[0]])
        count[0] += 1
        c.start()
        return c

    part = RB // 4
    edge_loads = [
        copy(A.in_edges.at[pl.ds(part * i, part)], A.edges_l.at[pl.ds(part * i, part)])
        for i in range(4)
    ]
    pairs = (
        (A.in_e, A.e_l),
        (A.in_i, A.i_l),
        (A.in_o, A.o_l),
        (A.in_m, A.m_l),
        (A.in_nodes, A.nodes_l),
        (A.in_gains, A.gains_l),
    )
    loads = [copy(*p) for p in pairs]
    stores = [copy(A.in_node_grad, A.o2), copy(A.in_edge_grad, A.o3)]
    for i in range(4):
        edge_loads[i].wait()

        @pl.loop(0, part // 16)
        def _(k, i=i):
            at = pl.ds(pl.multiple_of(part * i + 16 * k, 16), 16)
            A.edges_f[at] = A.edges_l[at].astype(F32)

        at = pl.ds(part * i, part)
        stores.append(copy(A.edges_f.at[at], A.o1.at[at]))
    for c in loads:
        c.wait()

    def widen(src, dst, out, rows):
        @pl.loop(0, rows // 16)
        def _(k):
            at = pl.ds(pl.multiple_of(16 * k, 16), 16)
            dst[at] = src[at].astype(F32)

        stores.append(copy(dst, out))

    widen(A.i_l, A.i_f, A.o7, D)
    widen(A.o_l, A.o_f, A.o8, S.FL)
    widen(A.nodes_l, A.nodes_f, A.o0, RB)
    widen(A.m_l, A.m_f, A.o4, 2 * D + DE)
    for u in range(4):
        row = 2 * D + DE + 128 * u
        A.mo_f[:, 128 * u : 128 * u + 128] = A.m_l[row : row + 128].astype(F32)
    stores.append(copy(A.mo_f, A.o5))
    mixed = A.e_l[9 * DE : 10 * DE].astype(F32)
    for t in range(9):
        A.ei_f[:, 128 * t : 128 * t + 128] = A.e_l[DE * t : DE * t + DE].astype(F32)
    A.ei_f[:, 1152 : 1152 + 64] = mixed[:, 0:64]
    stores.append(copy(A.ei_f, A.o10))
    A.eo_f[:, 0:128] = A.e_l[10 * DE : 11 * DE].astype(F32)
    A.eo_f[:, 128:DE] = pltpu.roll(mixed, 64, 1)[:, 0:64]
    stores.append(copy(A.eo_f, A.o11))
    A.ga_f[...] = A.gains_l[0:1]
    A.gb_f[...] = A.gains_l[1:2]
    A.gc_f[...] = A.gains_l[2:3, 0:DE]
    for src, out in ((A.ga_f, A.o6), (A.gb_f, A.o9), (A.gc_f, A.o12)):
        stores.append(copy(src, out))
    for c in stores:
        c.wait()


def unpack(S, values):
    D, DE, RB, RQ, K, FL = S.D, S.DE, S.RB, S.RQ, S.K, S.FL
    ins = ["in_nodes", "in_edges", "in_node_grad", "in_edge_grad"]
    ins += ["in_e", "in_i", "in_o", "in_m", "in_gains"]
    shapes = [
        (RB, D),
        (RB, K * DE),
        (RQ, D),
        (RQ, K * DE),
        (2 * D + DE, S.HM // 4),
        (S.HM // 4, D),
        (1, D),
        (D, FL),
        (FL, D),
        (1, D),
        (S.HE // 4, 2 * D + DE),
        (S.HE // 4, DE),
        (1, DE),
    ]
    outs = ["o%d" % i for i in range(13)]
    scratch = dict(
        edges_l=((RB, K * DE), BF16),
        edges_f=((RB, K * DE), F32),
        e_l=(values[4].shape, BF16),
        i_l=((D, FL), BF16),
        o_l=((FL, D), BF16),
        m_l=(values[7].shape, BF16),
        nodes_l=((RB, D), BF16),
        gains_l=((8, D), F32),
        i_f=((D, FL), F32),
        o_f=((FL, D), F32),
        nodes_f=((RB, D), F32),
        m_f=(shapes[4], F32),
        mo_f=(shapes[5], F32),
        ei_f=(shapes[10], F32),
        eo_f=(shapes[11], F32),
        ga_f=(shapes[6], F32),
        gb_f=(shapes[9], F32),
        gc_f=(shapes[12], F32),
    )
    names = ins + outs + list(scratch) + ["sems"]
    body = functools.partial(unpack_body, S, names)
    return list(
        pl.pallas_call(
            body,
            name="unpack",
            out_shape=[jax.ShapeDtypeStruct(x, F32) for x in shapes],
            in_specs=[ANY] * len(ins),
            out_specs=[ANY] * len(outs),
            scratch_shapes=[pltpu.VMEM(*v) for v in scratch.values()]
            + [pltpu.SemaphoreType.DMA((32,))],
            compiler_params=pltpu.CompilerParams(vmem_limit_bytes=62 * 1024 * 1024),
        )(*values)
    )


STOP = 0


def on_device(n_res, *args):
    nodes, edges, neighbours, _, _, _, _, ffn_in = args[:8]
    height = nodes.shape[0]
    degree = neighbours.shape[1]
    S = SimpleNamespace(
        n_res=n_res,
        bits=int(math.log2(n_res)),
        RB=height,
        RQ=height // 4,
        K=degree,
        D=nodes.shape[1],
        DE=edges.shape[1] // degree,
        HM=args[4].shape[1] * 4,
        HE=args[10].shape[1] * 4,
        FL=ffn_in.shape[1],
        grain=16 if n_res <= 16 else 8,
        remote=160,
        local=32,
        stop=STOP,
    )
    fixed = [a.reshape(1, -1) if a.ndim == 1 else a for a in args]
    for i in (2, 3, 10):
        fixed[i] = fixed[i].T
    out = unpack(S, build(S)(*fixed))
    for i in (6, 9, 12):
        out[i] = out[i].reshape(-1)
    out[10] = out[10].T
    return tuple(out)


def solution(mesh):
    in_specs = (
        P("res", None),
        P("res", None),
        P("res", None),
        P("res", None),
        P(None, "mp"),
        P("mp", None),
        P(),
        P(None, "mp"),
        P("mp", None),
        P(),
        P(None, "mp"),
        P("mp", None),
        P(),
        P("res", None),
        P("res", None),
    )
    out_specs = (
        P("res", None),
        P("res", None),
        P(("res", "mp"), None),
        P(("res", "mp"), None),
        P(None, "mp"),
        P("mp", None),
        P(),
        P(None, "mp"),
        P("mp", None),
        P(),
        P(None, "mp"),
        P("mp", None),
        P(),
    )
    return jax.shard_map(
        functools.partial(on_device, mesh.shape["res"]),
        mesh=mesh,
        in_specs=in_specs,
        out_specs=out_specs,
        check_vma=False,
    )
```

time: 991 us -> 246 us (0.25); the launches traced: 980 us -> 246 us
  waiting for transfers between devices: 438 us -> 0 us
  Pallas kernels: 0 us -> 245 us
  local copies, waits for them, and re-layouts: 206 us -> 0 us
  other arithmetic: 178 us -> 0 us
  matrix products: 90.2 us -> 0 us
  starting transfers between devices: 31.2 us -> 0 us
  blocking collectives: 20.8 us -> 0 us
  between operations: 15.3 us -> 0.82 us
    psum x9 -> x0, waiting for transfers between devices: 436 us -> none  [the longest x6 189 us: model_sum(): return lax.psum(values.astype(jnp.bfloat16), 'mp').astype(jnp.float32)]
    pallas_call x0 -> x2, Pallas kernels: none -> 245 us  [the longest x1 201 us: on_device(): out = unpack(S, build(S)(*fixed))]
    dot_general x35 -> x0, matrix products: 90.2 us -> none  [the longest x15 51.7 us: product(): return jnp.dot(left_side, right_side, preferred_element_type=jnp.float32)]
    scatter-add x2 -> x0, other arithmetic: 73.2 us -> none  [neighbour_back(): jax.ops.segment_sum(d_float, local_index, num_segments=3 * height)]
    reshape x10 -> x0, local copies, waits for them, and re-layouts: 53.5 us -> none  [the longest x2 16.1 us: on_device(): edge_flat = edges.reshape(edge_count, -1)]
    gather x4 -> x0, local copies, waits for them, and re-layouts: 52.2 us -> none  [neighbour_terms(): jnp.take(product(extended, other_weight), local_index, axis=0)]
    reduce_sum x20 -> x0, other arithmetic: 51.3 us -> none  [the longest x2 20.4 us: node_pass(): jnp.sum(smooth(before) * weights_mean[:, :, None], axis=1)]
    mul x8 -> x0, other arithmetic: 36.5 us -> none  [the longest x4 26.7 us: smooth(): return jax.nn.gelu(values, approximate=False)]
  transfers between devices with their start and end apart: 21 -> 0, of which waited for: 10 -> 0; matrix products, arithmetic and copies ran while one was open for 15% -> 0% of each run, Pallas kernels for 0% -> 0%
where the time goes in v1:
time: 246 us
  Pallas kernels  245 us (100%)
    pallas_call x1, Pallas kernels, on_device(): out = unpack(S, build(S)(*fixed))  201 us
    pallas_call x1, Pallas kernels, unpack(): pl.pallas_call(body, name='unpack', out_shape=[jax.ShapeDtypeStruct(x, F3...  44.6 us

profile of v1, /device:TPU:0, one launch (start us, length us, event | category | flops | bytes accessed | tf_op | source)
XLA Modules:
  0.0 246.2 jit_solution(14572647235973428359)
XLA Ops:
  0.7 200.8 %layer.1 = (bf16[192,512]{1,0:T(8,128)(2,1)}, bf16[192,6912]{1,0:T(8,128)(2,1)}, f32[48,512]{1,0:T(8,128)}, f32[48,6912]{1,0:T(8,128)}, bf16[2176,128]{1,0:T(8,1...) custom-call(f32[192,512]{1,0:T(8,128)} %refs_0_.1, ...), custom_call_target="tpu_custom_call" | custom-call | tf_op jit(solution)/shard_map/layer/pallas_call | solution.py:1251
  201.5 44.6 %unpack.1 = (f32[192,512]{1,0:T(8,128)}, f32[192,6912]{1,0:T(8,128)}, f32[48,512]{1,0:T(8,128)}, f32[48,6912]{1,0:T(8,128)}, f32[1216,128]{1,0:T(8,128)}, /*inde...) custom-call(bf16[192,512]{1,0:T(8,128)(2,1)} %get-tuple-element.35.r, ...), custom_call_target="tpu_custom_call" | custom-call | tf_op jit(solution)/shard_map/unpack/pallas_call | solution.py:1212

commit v2 on v1

--- a/solution.py
+++ b/solution.py
@@ -14,8 +14,7 @@
 BF16 = jnp.bfloat16
 MESH = pl.DeviceIdType.MESH
 ROOT_TWO_PI = 0.3989422804014327
-SCALE = 0.3275911 * 0.7071067811865476
-TAIL = (0.127414796, -0.142248368, 0.7107068705, -0.7265760135, 0.5307027145)
+ROOT_HALF = 0.7071067811865476
 ANY = pl.BlockSpec(memory_space=pl.ANY)
 VMEM = pl.BlockSpec(memory_space=pltpu.VMEM)
 
@@ -33,13 +32,11 @@
 
 
 def bell(v):
-    t = 1.0 / (1.0 + SCALE * jnp.abs(v))
-    fall = jnp.exp(-0.5 * (v * v))
-    poly = TAIL[4]
-    for c in (TAIL[3], TAIL[2], TAIL[1], TAIL[0]):
-        poly = c + t * poly
-    tail = t * poly * fall
-    return jnp.where(v >= 0.0, 1.0 - tail, tail), fall
+    return 0.5 + 0.5 * lax.erf(v * ROOT_HALF)
+
+
+def bell_slope(phi, v):
+    return phi + v * (jnp.exp(-0.5 * (v * v)) * ROOT_TWO_PI)
 
 
 def norm_parts(values, width):
@@ -169,8 +166,11 @@
 
     for d in (1, 2, 3):
         greet(mp=peer(d))
-    for s in range(S.bits):
+    for s in range(S.bits - 2):
         greet(res=across(s))
+    stride = S.n_res // 4
+    for d in (1, 2, 3):
+        greet(res=res + ((res // stride + d) % 4 - res // stride) * stride)
 
     @pl.when(has_l)
     def _():
@@ -181,7 +181,7 @@
         greet(res=res + 1)
 
     sides = (res + S.n_res - 1) // S.n_res + 1 - (res + 1) // S.n_res
-    pl.semaphore_wait(barrier, 3 + S.bits + sides)
+    pl.semaphore_wait(barrier, 6 + S.bits - 2 + sides)
 
     class Spread:
         def __init__(self, src, place):
@@ -345,6 +345,20 @@
             c.wait_recv()
 
     late = []
+
+    def lanes_at(q):
+        return pl.ds(pl.multiple_of(128 * q, 128), 128)
+
+    def spread_columns(src, dst):
+        copies = [
+            net.remote(src.at[:, lanes_at(peer(d))], dst.at[quarter(mp)], mp=peer(d))
+            for d in (1, 2, 3)
+        ]
+        for c in copies:
+            c.start()
+        late.extend(copies)
+        dst[quarter(mp)] = src[:, lanes_at(mp)]
+        return copies
 
     def return_rows(product, send, recv, side_send, side_recv, fill, between):
         for blk in range(3):
@@ -447,7 +461,6 @@
         A.XT[256:768, at] = A.XO[at].T
 
     spread_msg_in.forward()
-    spread_msg_out.forward()
     halo.wait()
 
     gain_a = A.gain_a[...]
@@ -479,9 +492,9 @@
                     v = A.base[rows_at(RQ * k + 16 * sub, 16), 0:HM] + mine
                     at = rows_at(EC * c + RQ * k + 16 * sub, 16)
                     w = jnp.concatenate([A.WB[at]] * (HM // 128), axis=1)
-                    phi, fall = bell(v)
+                    phi = bell(v)
                     if keep:
-                        A.slope[at] = (w * (phi + v * fall * ROOT_TWO_PI)).astype(BF16)
+                        A.slope[at] = (w * bell_slope(phi, v)).astype(BF16)
                     total = total + w * (v * phi)
                 A.total[own] = total
 
@@ -500,10 +513,10 @@
         def _(i):
             rows = rows_at(16 * i, 16)
             v = A.hid[rows]
-            phi, fall = bell(v)
+            phi = bell(v)
             A.smooth[rows] = (v * phi).astype(BF16)
             if keep:
-                A.hslope[rows] = phi + v * fall * ROOT_TWO_PI
+                A.hslope[rows] = bell_slope(phi, v)
 
         A.part[...] = dot(A.smooth[...], A.fo_v[...])
         part_b[...] = A.part[...].astype(BF16)
@@ -527,6 +540,7 @@
     A.T[0:DE] = A.Wm[2 * D : 2 * D + DE]
     node_table(A.win1)
     message_mean(A.win1, False)
+    spread_msg_out.forward()
     spread_msg_out.wait()
     load_ffn_in.wait()
     load_ffn_out.wait()
@@ -545,6 +559,7 @@
     spread_edge[1].forward()
     node_table(A.win2)
     message_mean(A.win2, True)
+    move_avg = spread_columns(A.avg, A.avg_all)
     spread_edge[2].forward()
     spread_edge[3].forward()
     settled = node_tail(A.mixed[...], A.ug2, A.pb2, A.pr2, True)
@@ -600,7 +615,7 @@
             base = A.base[at] + A.selfe[rows_at(16 * (b % (RQ // 16)), 16)]
             A.base[at] = base
             v = base + A.pre2[at]
-            phi, _ = bell(v)
+            phi = bell(v)
             A.G[at] = (v * phi).astype(BF16)
 
         A.upd[...] = dot(A.G[...], A.Eop[...])
@@ -621,9 +636,9 @@
         def _(b):
             at = rows_at(16 * b, 16)
             v = A.base[at] + A.pre2[at]
-            phi, fall = bell(v)
+            phi = bell(v)
             A.G2[rows_at(EC * c + 16 * b, 16)] = (v * phi).astype(BF16)
-            A.base[at] = phi + v * fall * ROOT_TWO_PI
+            A.base[at] = bell_slope(phi, v)
 
         A.upd[...] = dot(A.G2[rows], A.Eop[...])
         for j in range(3):
@@ -676,6 +691,19 @@
     on_last = net.remote(new_part(cross, chunks - 1), new_part(cross, chunks - 1), mp=pair)
 
     A.dself_low[...] = A.dself[...].astype(BF16)
+    for q in range(4):
+        more = A.dself[:, 4 * big + 128 * (q // 2) : 4 * big + 128 * (q // 2) + 128]
+        if q % 2:
+            more = pltpu.roll(more, 64, 1)
+        A.ds_send[q, :, 0:128] = A.dself_low[:, 128 * q : 128 * q + 128]
+        A.ds_send[q, :, 128:256] = more.astype(BF16)
+    move_ds = [
+        net.remote(A.ds_send.at[peer(d)], A.ds_all.at[quarter(mp)], mp=peer(d)) for d in (1, 2, 3)
+    ]
+    for c in move_ds:
+        c.start()
+    late.extend(move_ds)
+    A.ds_all[quarter(mp)] = A.ds_send[mp]
     for blk in range(3):
         at = slice(RB * blk, RB * blk + RB)
         A.dq[at] = dot(A.XT[DE + RB * blk : DE + RB * blk + RB], A.DP2[...]).astype(BF16)
@@ -697,36 +725,41 @@
     def edge_weight_gradients():
         by_in = dot_at(A.XM[...], A.DP2[...])
         by_out = dot_at(A.DO[...], A.G2[...])
-        emit_edge(8, jnp.transpose(by_in[0:128]))
-        emit_edge(10, jnp.transpose(by_out[0:128]))
+        emit_edge(4, jnp.transpose(by_in[0:128]))
+        emit_edge(6, jnp.transpose(by_out[0:128]))
         emit_edge(
-            9, jnp.transpose(jnp.concatenate([by_in[128:DE], by_out[128:DE]], axis=0))
+            5, jnp.transpose(jnp.concatenate([by_in[128:DE], by_out[128:DE]], axis=0))
         )
-        own = A.win3[quarter(mp, RB)]
         for t in range(4):
             at = slice(128 * t, 128 * t + 128)
-            emit_edge(t, jnp.transpose(dot_at(own[:, at], A.dself_low[...])))
-            emit_edge(4 + t, jnp.transpose(dot_at(A.win3[:, at], A.dq[...])))
+            emit_edge(t, jnp.transpose(dot_at(A.win3[:, at], A.dq[...])))
         pump(sum_edge)
+        landed(move_ds)
+        value = dot_at(A.ds_all[...], A.win3[RB : 2 * RB])
+        for t in range(4):
+            A.work_e[DE * t : DE * t + DE] = value[0:DE, 128 * t : 128 * t + 128].astype(BF16)
 
     def message_weight_gradients():
-        own = A.win2[quarter(mp, RB)]
         for t in range(4):
             at = slice(128 * t, 128 * t + 128)
-            emit_msg(128 * t, dot_at(own[:, at], A.dmsg_low[...]))
-            emit_msg(D + 128 * t, dot_at(A.win2[:, at], A.dq1[...]))
-            value = dot_at(A.avg[:, at], A.dg1[...])
-            for u in range(4):
-                row = 2 * D + DE + 128 * u
-                A.gm[t, row : row + 128] = value[:, 128 * u : 128 * u + 128].astype(BF16)
-        emit_msg(2 * D, dot(A.XT[0:DE], A.DP[...]))
-
-    for ref, used in ((A.ge, 11 * DE), (A.gm, 3 * D + DE)):
-        if ref.shape[1] > used:
-            for q in range(4):
-                ref[q, used:] = jnp.zeros((ref.shape[1] - used, 128), BF16)
-
-    def reduce_mp(g, got, cuts):
+            emit_msg(128 * t, dot_at(A.win2[:, at], A.dq1[...]))
+        emit_msg(D, dot(A.XT[0:DE], A.DP[...]))
+
+    def own_message_gradients():
+        landed(move_avg)
+        landed(move_dg1)
+        landed(move_dmsg)
+        A.work_m[0:D] = dot_at(A.win2[RB : 2 * RB], A.dmsg_all[...]).astype(BF16)
+        value = dot_at(A.avg_all[...], A.dg1_all[...])
+        for u in range(4):
+            row = 2 * D + DE + 128 * u
+            A.work_m[row : row + 128] = value[:, 128 * u : 128 * u + 128].astype(BF16)
+
+    for ref, used in ((A.work_e, 11 * DE), (A.work_m, 3 * D + DE)):
+        if ref.shape[0] > used:
+            ref[used:] = jnp.zeros((ref.shape[0] - used, 128), BF16)
+
+    def reduce_mp(g, got, cuts, work, base):
         rows = g.shape[1]
         a1 = net.remote(g.at[pair], got.at[0], mp=pair)
         a2 = net.remote(g.at[third], got.at[1], mp=pair)
@@ -755,16 +788,17 @@
         def _(i):
             at = rows_at(32 * i, 32)
             total = g[mp, at].astype(F32) + got[0, at].astype(F32) + got[2, at].astype(F32)
-            got[0, at] = total.astype(BF16)
+            work[rows_at(base + 32 * i, 32)] = total.astype(BF16)
 
         for c in (a1, a2, *pieces):
             c.wait_send()
 
-    def reduce_res(work, got, out, result, order):
+    def reduce_res(work, got, out, result):
         size = work.shape[0]
         low = 0
         used = 0
-        for s in order:
+        halvings = range(S.bits - 2)
+        for s in halvings:
             bit = (res // (1 << s)) % 2
             size = size // 2
             keep = low + bit * size
@@ -775,17 +809,51 @@
             c.start()
             yield
             c.wait()
-            into = out if s == order[-1] else work
 
             @pl.loop(0, size // S.grain)
-            def _(i, keep=keep, used=used, into=into):
+            def _(i, keep=keep, used=used):
                 at = rows_at(keep + S.grain * i, S.grain, S.grain)
                 there = rows_at(used + S.grain * i, S.grain, S.grain)
-                into[at] = (work[at].astype(F32) + got[there].astype(F32)).astype(BF16)
+                work[at] = (work[at].astype(F32) + got[there].astype(F32)).astype(BF16)
 
             used += size
             low = keep
-        for s in reversed(order):
+        me = res // stride
+        size = size // 4
+        copies = []
+        for d in (2, 1, 3):
+            there = (me + d) % 4
+            c = net.remote(
+                work.at[rows_at(low + there * size, size, S.grain)],
+                got.at[pl.ds(used + (d - 1) * size, size)],
+                res=res + (there - me) * stride,
+            )
+            c.start()
+            copies.append(c)
+        yield
+        for c in copies:
+            c.wait()
+        own = low + me * size
+
+        @pl.loop(0, size // S.grain)
+        def _(i):
+            at = rows_at(own + S.grain * i, S.grain, S.grain)
+            total = work[at].astype(F32)
+            for d in range(3):
+                total = total + got[rows_at(used + d * size + S.grain * i, S.grain, S.grain)].astype(F32)
+            out[at] = total.astype(BF16)
+
+        here = out.at[rows_at(own, size, S.grain)]
+        copies = []
+        for d in (2, 1, 3):
+            c = net.remote(here, here, res=res + ((me + d) % 4 - me) * stride)
+            c.start()
+            copies.append(c)
+        yield
+        for c in copies:
+            c.wait()
+        size = 4 * size
+        for s in reversed(halvings):
             bit = (res // (1 << s)) % 2
             here = out.at[rows_at(low, size, S.grain)]
             c = net.remote(here, here, res=across(s))
@@ -820,14 +888,15 @@
         for g in sums:
             next(g, None)
 
-    order = list(range(S.bits))
     sum_edge = chain(
-        reduce_mp(A.ge, A.ge_r, 2), reduce_res(A.ge_r.at[0], A.sum_er, A.sum_e, A.pack_e, order)
-    )
-    sum_in = reduce_res(A.grad_i, A.sum_ir, A.sum_i, A.pack_i, order)
-    sum_out = reduce_res(A.grad_o, A.sum_or, A.sum_o, A.pack_o, order)
+        reduce_mp(A.ge, A.ge_r, 2, A.work_e, 4 * DE),
+        reduce_res(A.work_e, A.sum_er, A.sum_e, A.pack_e),
+    )
+    sum_in = reduce_res(A.grad_i, A.sum_ir, A.sum_i, A.pack_i)
+    sum_out = reduce_res(A.grad_o, A.sum_or, A.sum_o, A.pack_o)
     sum_msg = chain(
-        reduce_mp(A.gm, A.gm_r, 1), reduce_res(A.gm_r.at[0], A.sum_mr, A.sum_m, A.pack_m, order)
+        reduce_mp(A.gm, A.gm_r, 1, A.work_m, D),
+        reduce_res(A.work_m, A.sum_mr, A.sum_m, A.pack_m),
     )
     sum_gains = reduce_gains()
 
@@ -880,6 +949,9 @@
     pump(sum_gains)
     A.dsa[...] = d_sum_a
     A.dg1[...] = d_sum_a.astype(BF16)
+    A.dg1_all[quarter(mp)] = A.dg1[...]
+    move_dg1 = gather_rows(A.dg1_all)
+    late.extend(move_dg1)
     A.davg[...] = dot_bt(A.dg1[...], A.Wo[...])
 
     for sub in range(RQ // 16):
@@ -894,15 +966,19 @@
         total = lax.fori_loop(0, K, back_step, jnp.zeros((16, HM), F32))
         A.dmsg_low[16 * sub : 16 * sub + 16] = total.astype(BF16)
 
+    move_dmsg = spread_columns(A.dmsg_low, A.dmsg_all)
+    pump(sum_edge)
     for blk in range(3):
         at = slice(RB * blk, RB * blk + RB)
         A.dq1[at] = dot(A.XT[DE + RB * blk : DE + RB * blk + RB], A.DP[...]).astype(BF16)
 
     message_weight_gradients()
-    pump(sum_msg, sum_edge, sum_in, sum_out, sum_gains)
-
-    def edge_gradient():
-        @pl.loop(0, E // EC)
+    pump(sum_msg, sum_in, sum_gains)
+    own_message_gradients()
+    pump(sum_msg)
+
+    def edge_gradient(start, stop):
+        @pl.loop(start, stop)
         def _(c):
             rows = rows_at(EC * c, EC)
             A.EG[rows] = A.EG[rows] + dot_bt(A.DP[rows], A.T[0:256])
@@ -914,6 +990,7 @@
                 ]
                 pair_store(A.ec_v, lanes, ends[0], ends[1])
 
+    def close_edges():
         store.append(net.copy(A.ec_v, A.out_edge_grad))
         for a, b, c in streams:
             a.wait()
@@ -925,8 +1002,11 @@
         store.append(net.copy(A.new_edges, A.out_edges))
 
     def fill_b():
-        pump(sum_msg)
-        edge_gradient()
+        edge_gradient(0, 3)
+        pump(sum_out, sum_gains)
+        edge_gradient(3, chunks)
+        close_edges()
+        pump(sum_msg, sum_edge, sum_in)
 
     back = return_rows(
         lambda blk: dot_bt(A.dq1[RB * blk : RB * blk + RB], A.Wm[D : 2 * D]),
@@ -935,7 +1015,7 @@
         A.back_side_send_b,
         A.back_side_b,
         fill_b,
-        lambda: pump(sum_in, sum_out, sum_edge, sum_msg, sum_gains),
+        lambda: pump(sum_out, sum_gains),
     )
     A.node_grad_v[...] = 0.5 * (A.dsa[...] + dot_bt(A.dmsg_low[...], A.Wm[0:D]) + back)
     store.append(net.copy(A.node_grad_v, A.out_node_grad))
@@ -1057,8 +1137,14 @@
         DP=((E, S.HM), BF16),
         dmsg_low=((S.RQ, S.HM), BF16),
         dq1=((W, S.HM), BF16),
-        ge=((4, rows_e, 128), BF16),
-        ge_r=((3, rows_e, 128), BF16),
+        ge=((4, 7 * S.DE, 128), BF16),
+        ge_r=((3, 7 * S.DE, 128), BF16),
+        work_e=((rows_e, 128), BF16),
+        ds_send=((4, S.RQ, 256), BF16),
+        ds_all=((S.RB, 256), BF16),
+        avg_all=((S.RB, 128), BF16),
+        dg1_all=((S.RB, S.D), BF16),
+        dmsg_all=((S.RB, 128), BF16),
         sum_er=((rows_e, 128), BF16),
         sum_e=((rows_e, 128), BF16),
         grad_i=((S.D, S.FL), BF16),
@@ -1067,8 +1153,9 @@
         grad_o=((S.FL, S.D), BF16),
         sum_or=((S.FL, S.D), BF16),
         sum_o=((S.FL, S.D), BF16),
-        gm=((4, rows_m, 128), BF16),
-        gm_r=((3, rows_m, 128), BF16),
+        gm=((4, S.D + S.DE, 128), BF16),
+        gm_r=((3, S.D + S.DE, 128), BF16),
+        work_m=((rows_m, 128), BF16),
         sum_mr=((rows_m, 128), BF16),
         sum_m=((rows_m, 128), BF16),
     )
@@ -1119,7 +1206,8 @@
         (A.in_gains, A.gains_l),
     )
     loads = [copy(*p) for p in pairs]
-    stores = [copy(A.in_node_grad, A.o2), copy(A.in_edge_grad, A.o3)]
+    grads = [copy(A.in_edge_grad, A.eg_l), copy(A.in_node_grad, A.ng_l)]
+    stores = []
     for i in range(4):
         edge_loads[i].wait()
 
@@ -1130,8 +1218,9 @@
 
         at = pl.ds(part * i, part)
         stores.append(copy(A.edges_f.at[at], A.o1.at[at]))
-    for c in loads:
+    for c in (*grads, *loads):
         c.wait()
+    stores += [copy(A.eg_l, A.o3), copy(A.ng_l, A.o2)]
 
     def widen(src, dst, out, rows):
         @pl.loop(0, rows // 16)
@@ -1195,6 +1284,8 @@
         m_l=(values[7].shape, BF16),
         nodes_l=((RB, D), BF16),
         gains_l=((8, D), F32),
+        eg_l=((RQ, K * DE), F32),
+        ng_l=((RQ, D), F32),
         i_f=((D, FL), F32),
         o_f=((FL, D), F32),
         nodes_f=((RB, D), F32),
@@ -1241,7 +1332,7 @@
         HE=args[10].shape[1] * 4,
         FL=ffn_in.shape[1],
         grain=16 if n_res <= 16 else 8,
-        remote=160,
+        remote=200,
         local=32,
         stop=STOP,
     )

time: 246 us -> 194 us (0.79)
  Pallas kernels: 245 us -> 193 us
    pallas_call x1, Pallas kernels: 44.6 us -> 7.34 us  [unpack(): pl.pallas_call(body, name='unpack', out_shape=[jax.ShapeDtypeStruct(x, F3...]
    pallas_call x1, Pallas kernels: 201 us -> 185 us  [on_device(): out = unpack(S, build(S)(*fixed))]
where the time goes in v2:
time: 194 us; the launch traced here: 193 us
  Pallas kernels  193 us (99%)
    pallas_call x1, Pallas kernels, on_device(): out = unpack(S, build(S)(*fixed))  185 us
    pallas_call x1, Pallas kernels, unpack(): pl.pallas_call(body, name='unpack', out_shape=[jax.ShapeDtypeStruct(x, F3...  7.34 us

profile of v2, /device:TPU:0, one launch (start us, length us, event | category | flops | bytes accessed | tf_op | source)
XLA Modules:
  0.0 193.4 jit_solution(15635015327035052677)
XLA Ops:
  0.7 185.2 %layer.1 = (bf16[192,512]{1,0:T(8,128)(2,1)}, bf16[192,6912]{1,0:T(8,128)(2,1)}, f32[48,512]{1,0:T(8,128)}, f32[48,6912]{1,0:T(8,128)}, bf16[2176,128]{1,0:T(8,1...) custom-call(f32[192,512]{1,0:T(8,128)} %refs_0_.1, ...), custom_call_target="tpu_custom_call" | custom-call | tf_op jit(solution)/shard_map/layer/pallas_call | solution.py:1342
  185.9 7.3 %unpack.1 = (f32[192,512]{1,0:T(8,128)}, f32[192,6912]{1,0:T(8,128)}, f32[48,512]{1,0:T(8,128)}, f32[48,6912]{1,0:T(8,128)}, f32[1216,128]{1,0:T(8,128)}, /*inde...) custom-call(bf16[192,512]{1,0:T(8,128)(2,1)} %get-tuple-element.35.r, ...), custom_call_target="tpu_custom_call" | custom-call | tf_op jit(solution)/shard_map/unpack/pallas_call | solution.py:1303

commit v3 on v2

--- a/solution.py
+++ b/solution.py
@@ -56,6 +56,14 @@
 
 def up(rows, step):
     return -(-rows // step) * step
+
+
+def unrolled(count):
+    def run(step):
+        for i in range(count):
+            step(i)
+
+    return run
 
 
 class Net:
@@ -396,7 +404,7 @@
     spread_msg_out.start()
     load_nodes.wait()
 
-    @pl.loop(0, RB // 16)
+    @unrolled(RB // 16)
     def _(i):
         A.win1[rows_at(RB + 16 * i, 16)] = A.nodes_v[rows_at(16 * i, 16)].astype(BF16)
 
@@ -481,20 +489,21 @@
         def _(c):
             rows = rows_at(EC * c, EC)
             left = jnp.concatenate([A.XE[rows], A.XO[rows]], axis=1)
-            A.base[:, 0:HM] = dot(left, A.T[...])
-
-            @pl.loop(0, RQ // 16)
+            A.pre[...] = dot(left, A.T[...])
+
+            @unrolled(RQ // 16)
             def _(sub):
-                own = rows_at(16 * sub, 16)
+                own = slice(16 * sub, 16 * sub + 16)
                 mine = A.selfs[own]
                 total = A.total[own]
                 for k in range(6):
-                    v = A.base[rows_at(RQ * k + 16 * sub, 16), 0:HM] + mine
-                    at = rows_at(EC * c + RQ * k + 16 * sub, 16)
-                    w = jnp.concatenate([A.WB[at]] * (HM // 128), axis=1)
+                    at = RQ * k + 16 * sub
+                    v = A.pre[at : at + 16] + mine
+                    there = rows_at(EC * c + at, 16)
+                    w = jnp.concatenate([A.WB[there]] * (HM // 128), axis=1)
                     phi = bell(v)
                     if keep:
-                        A.slope[at] = (w * bell_slope(phi, v)).astype(BF16)
+                        A.slope[there] = (w * bell_slope(phi, v)).astype(BF16)
                     total = total + w * (v * phi)
                 A.total[own] = total
 
@@ -509,7 +518,7 @@
         late.extend(moved)
         A.hid[...] = dot(ug[...], A.fi_v[...])
 
-        @pl.loop(0, RB // 16)
+        @unrolled(RB // 16)
         def _(i):
             rows = rows_at(16 * i, 16)
             v = A.hid[rows]
@@ -604,43 +613,52 @@
             make(stream + 2 * chunks + c, new_part(cross, c), new_part(cross, c), mp=pair),
         )
 
-    def edge_chunk(c, gain_total):
+    def edge_chunk(c, part, gain_out):
         rows = rows_at(EC * c, EC)
-        A.base[...] = dot(A.XO[rows], A.Te[256:768])
-        A.pre2[...] = dot(A.XE[rows], A.Te[0:256])
-
-        @pl.loop(0, EC // 16)
+        base, pre2, upd, emix, G = (x.at[part] for x in (A.base, A.pre2, A.upd, A.emix, A.G))
+        base[...] = dot(A.XO[rows], A.Te[256:768])
+        pre2[...] = dot(A.XE[rows], A.Te[0:256])
+        yield
+
+        @unrolled(EC // 16)
         def _(b):
-            at = rows_at(16 * b, 16)
-            base = A.base[at] + A.selfe[rows_at(16 * (b % (RQ // 16)), 16)]
-            A.base[at] = base
-            v = base + A.pre2[at]
-            phi = bell(v)
-            A.G[at] = (v * phi).astype(BF16)
-
-        A.upd[...] = dot(A.G[...], A.Eop[...])
+            at = slice(16 * b, 16 * b + 16)
+            own = 16 * (b % (RQ // 16))
+            total = base[at] + A.selfe[own : own + 16]
+            base[at] = total
+            v = total + pre2[at]
+            G[at] = (v * bell(v)).astype(BF16)
+
+        yield
+        upd[...] = dot(G[...], A.Eop[...])
+        yield
         for j in range(3):
             both = pair_load(A.e_v, pl.multiple_of(1152 * c + 384 * j, 128))
             for p in range(2):
                 k = 2 * j + p
                 mine = slice(RQ * k, RQ * k + RQ)
                 at = rows_at(EC * c + RQ * k, RQ)
-                normed, _ = norm_parts_e(both[p] + A.upd[mine])
+                normed, _ = norm_parts_e(both[p] + upd[mine])
                 mixed = 0.5 * (both[p] + normed * gain_c)
-                A.emix[mine] = mixed
+                emix[mine] = mixed
                 A.XM[at] = jnp.where(is_edge, mixed, A.XE[at].astype(F32)).astype(BF16)
 
-        A.pre2[...] = dot(A.XM[rows], A.Te[0:256])
-
-        @pl.loop(0, EC // 16)
+        yield
+        pre2[...] = dot(A.XM[rows], A.Te[0:256])
+        yield
+
+        @unrolled(EC // 16)
         def _(b):
-            at = rows_at(16 * b, 16)
-            v = A.base[at] + A.pre2[at]
+            at = slice(16 * b, 16 * b + 16)
+            v = base[at] + pre2[at]
             phi = bell(v)
             A.G2[rows_at(EC * c + 16 * b, 16)] = (v * phi).astype(BF16)
-            A.base[at] = bell_slope(phi, v)
-
-        A.upd[...] = dot(A.G2[rows], A.Eop[...])
+            base[at] = bell_slope(phi, v)
+
+        yield
+        upd[...] = dot(A.G2[rows], A.Eop[...])
+        yield
+        gain_total = jnp.zeros((8, 256), F32)
         for j in range(3):
             lanes = pl.multiple_of(1152 * c + 384 * j, 128)
             cots = pair_load(A.ec_v, lanes)
@@ -648,16 +666,35 @@
             for p in range(2):
                 k = 2 * j + p
                 mine = slice(RQ * k, RQ * k + RQ)
-                normed, inverse = norm_parts_e(A.emix[mine] + A.upd[mine])
+                normed, inverse = norm_parts_e(emix[mine] + upd[mine])
                 news.append(normed * gain_c)
                 gain_total = gain_total + jnp.sum(
                     (cots[p] * normed).reshape(RQ // 8, 8, 256), axis=0
                 )
                 d_sum = jnp.where(is_edge, norm_back(cots[p], normed, inverse, gain_c, DE), 0.0)
-                A.emix[mine] = d_sum
+                emix[mine] = d_sum
                 A.DO[rows_at(EC * c + RQ * k, RQ)] = d_sum.astype(BF16)
             pair_store(A.new_edges, lanes, news[0], news[1], quarter(mp))
-
+        gain_out.append(gain_total)
+        yield
+        pre2[...] = dot_bt(A.DO[rows], A.Eop[...])
+        yield
+
+        @unrolled(RQ // 16)
+        def _(sub):
+            own = slice(16 * sub, 16 * sub + 16)
+            total = A.dself[own]
+            for k in range(6):
+                at = slice(RQ * k + 16 * sub, RQ * k + 16 * sub + 16)
+                d = (pre2[at] * base[at]).astype(BF16)
+                A.DP2[rows_at(EC * c + RQ * k + 16 * sub, 16)] = d
+                total = total + d.astype(F32)
+            A.dself[own] = total
+
+        yield
+        A.EG[rows] = 0.5 * (emix[...] + dot_bt(A.DP2[rows], A.Te[0:256]))
+
+    def send_chunk(c):
         to_pair, to_cross, _ = stream_copies(net.at, c)
         to_cross.start()
         to_pair.start()
@@ -668,21 +705,22 @@
             arrived.wait_recv()
             on.start()
 
-
-        A.pre2[...] = dot_bt(A.DO[rows], A.Eop[...])
-
-        @pl.loop(0, EC // 16)
-        def _(b):
-            at = rows_at(16 * b, 16)
-            own = rows_at(16 * (b % (RQ // 16)), 16)
-            d = (A.pre2[at] * A.base[at]).astype(BF16)
-            A.DP2[rows_at(EC * c + 16 * b, 16)] = d
-            A.dself[own] = A.dself[own] + d.astype(F32)
-
-        A.EG[rows] = 0.5 * (A.emix[...] + dot_bt(A.DP2[rows], A.Te[0:256]))
-        return gain_total
-
-    gain_total = lax.fori_loop(0, E // EC, edge_chunk, jnp.zeros((8, 256), F32))
+    def edge_chunks(i, gain_total):
+        gains = []
+        parts = [edge_chunk(2 * i + h, h, gains) for h in range(2)]
+        next(parts[0])
+        running = list(parts)
+        while running:
+            for g in list(running):
+                try:
+                    next(g)
+                except StopIteration:
+                    running.remove(g)
+        for h in range(2):
+            send_chunk(2 * i + h)
+        return gain_total + gains[0] + gains[1]
+
+    gain_total = lax.fori_loop(0, chunks // 2, edge_chunks, jnp.zeros((8, 256), F32))
     A.gains[...] = jnp.zeros_like(A.gains)
     A.gains[2:3, 0:256] = jnp.sum(gain_total, axis=0, keepdims=True)
 
@@ -793,75 +831,74 @@
         for c in (a1, a2, *pieces):
             c.wait_send()
 
-    def reduce_res(work, got, out, result):
+    def reduce_res(work, got, out, result, plan):
         size = work.shape[0]
         low = 0
         used = 0
-        halvings = range(S.bits - 2)
-        for s in halvings:
-            bit = (res // (1 << s)) % 2
-            size = size // 2
-            keep = low + bit * size
-            give = low + (1 - bit) * size
-            c = net.remote(
-                work.at[rows_at(give, size, S.grain)], got.at[pl.ds(used, size)], res=across(s)
-            )
-            c.start()
+        me = res // stride
+        grain = S.grain
+        for n, s in enumerate(plan):
+            into = out if n == len(plan) - 1 else work
+            if s >= 0:
+                bit = (res // (1 << s)) % 2
+                size = size // 2
+                keep = low + bit * size
+                give = low + (1 - bit) * size
+                copies = [
+                    net.remote(
+                        work.at[rows_at(give, size, grain)],
+                        got.at[pl.ds(used, size)],
+                        res=across(s),
+                    )
+                ]
+            else:
+                size = size // 4
+                keep = low + me * size
+                copies = []
+                for d in (2, 1, 3):
+                    there = (me + d) % 4
+                    copies.append(
+                        net.remote(
+                            work.at[rows_at(low + there * size, size, grain)],
+                            got.at[pl.ds(used + (d - 1) * size, size)],
+                            res=res + (there - me) * stride,
+                        )
+                    )
+            for c in copies:
+                c.start()
             yield
-            c.wait()
-
-            @pl.loop(0, size // S.grain)
-            def _(i, keep=keep, used=used):
-                at = rows_at(keep + S.grain * i, S.grain, S.grain)
-                there = rows_at(used + S.grain * i, S.grain, S.grain)
-                work[at] = (work[at].astype(F32) + got[there].astype(F32)).astype(BF16)
-
-            used += size
+            for c in copies:
+                c.wait()
+
+            @pl.loop(0, size // grain)
+            def _(i, keep=keep, used=used, into=into, terms=len(copies), size=size):
+                at = rows_at(keep + grain * i, grain, grain)
+                total = work[at].astype(F32)
+                for d in range(terms):
+                    total = total + got[rows_at(used + d * size + grain * i, grain, grain)].astype(F32)
+                into[at] = total.astype(BF16)
+
+            used += size * len(copies)
             low = keep
-        me = res // stride
-        size = size // 4
-        copies = []
-        for d in (2, 1, 3):
-            there = (me + d) % 4
-            c = net.remote(
-                work.at[rows_at(low + there * size, size, S.grain)],
-                got.at[pl.ds(used + (d - 1) * size, size)],
-                res=res + (there - me) * stride,
-            )
-            c.start()
-            copies.append(c)
-        yield
-        for c in copies:
-            c.wait()
-        own = low + me * size
-
-        @pl.loop(0, size // S.grain)
-        def _(i):
-            at = rows_at(own + S.grain * i, S.grain, S.grain)
-            total = work[at].astype(F32)
-            for d in range(3):
-                total = total + got[rows_at(used + d * size + S.grain * i, S.grain, S.grain)].astype(F32)
-            out[at] = total.astype(BF16)
-
-        here = out.at[rows_at(own, size, S.grain)]
-        copies = []
-        for d in (2, 1, 3):
-            c = net.remote(here, here, res=res + ((me + d) % 4 - me) * stride)
-            c.start()
-            copies.append(c)
-        yield
-        for c in copies:
-            c.wait()
-        size = 4 * size
-        for s in reversed(halvings):
-            bit = (res // (1 << s)) % 2
-            here = out.at[rows_at(low, size, S.grain)]
-            c = net.remote(here, here, res=across(s))
-            c.start()
+        for s in reversed(plan):
+            here = out.at[rows_at(low, size, grain)]
+            if s >= 0:
+                copies = [net.remote(here, here, res=across(s))]
+                low = low - (res // (1 << s)) % 2 * size
+                grow = 2
+            else:
+                copies = [
+                    net.remote(here, here, res=res + ((me + d) % 4 - me) * stride)
+                    for d in (2, 1, 3)
+                ]
+                low = low - me * size
+                grow = 4
+            for c in copies:
+                c.start()
             yield
-            c.wait()
-            low = low - bit * size
-            size = 2 * size
+            for c in copies:
+                c.wait()
+            size = grow * size
         store.append(net.copy(out, result))
 
     def reduce_gains():
@@ -890,13 +927,13 @@
 
     sum_edge = chain(
         reduce_mp(A.ge, A.ge_r, 2, A.work_e, 4 * DE),
-        reduce_res(A.work_e, A.sum_er, A.sum_e, A.pack_e),
-    )
-    sum_in = reduce_res(A.grad_i, A.sum_ir, A.sum_i, A.pack_i)
-    sum_out = reduce_res(A.grad_o, A.sum_or, A.sum_o, A.pack_o)
+        reduce_res(A.work_e, A.sum_er, A.sum_e, A.pack_e, plans(S.bits)[0]),
+    )
+    sum_in = reduce_res(A.grad_i, A.sum_ir, A.sum_i, A.pack_i, plans(S.bits)[1])
+    sum_out = reduce_res(A.grad_o, A.sum_or, A.sum_o, A.pack_o, plans(S.bits)[2])
     sum_msg = chain(
         reduce_mp(A.gm, A.gm_r, 1, A.work_m, D),
-        reduce_res(A.work_m, A.sum_mr, A.sum_m, A.pack_m),
+        reduce_res(A.work_m, A.sum_mr, A.sum_m, A.pack_m, plans(S.bits)[3]),
     )
     sum_gains = reduce_gains()
 
@@ -925,7 +962,7 @@
     late.extend(moved)
     A.hid[...] = dot_bt(A.dF[...], A.fo_v[...])
 
-    @pl.loop(0, RB // 16)
+    @unrolled(RB // 16)
     def _(i):
         rows = rows_at(16 * i, 16)
         A.dT[rows] = (A.hid[rows] * A.hslope[rows]).astype(BF16)
@@ -972,8 +1009,9 @@
         at = slice(RB * blk, RB * blk + RB)
         A.dq1[at] = dot(A.XT[DE + RB * blk : DE + RB * blk + RB], A.DP[...]).astype(BF16)
 
+    pump(sum_in, sum_out)
     message_weight_gradients()
-    pump(sum_msg, sum_in, sum_gains)
+    pump(sum_msg, sum_gains)
     own_message_gradients()
     pump(sum_msg)
 
@@ -1003,10 +1041,9 @@
 
     def fill_b():
         edge_gradient(0, 3)
-        pump(sum_out, sum_gains)
+        pump(sum_in, sum_out, sum_gains)
         edge_gradient(3, chunks)
-        close_edges()
-        pump(sum_msg, sum_edge, sum_in)
+        pump(sum_msg, sum_edge)
 
     back = return_rows(
         lambda blk: dot_bt(A.dq1[RB * blk : RB * blk + RB], A.Wm[D : 2 * D]),
@@ -1015,12 +1052,14 @@
         A.back_side_send_b,
         A.back_side_b,
         fill_b,
-        lambda: pump(sum_out, sum_gains),
+        lambda: pump(sum_in, sum_out, sum_gains),
     )
     A.node_grad_v[...] = 0.5 * (A.dsa[...] + dot_bt(A.dmsg_low[...], A.Wm[0:D]) + back)
     store.append(net.copy(A.node_grad_v, A.out_node_grad))
 
-    work = [sum_in, sum_out, sum_edge, sum_msg, sum_gains]
+    pump(sum_edge, sum_msg)
+    close_edges()
+    work = [sum_msg, sum_edge, sum_in, sum_out, sum_gains]
     while work:
         for g in list(work):
             try:
@@ -1106,11 +1145,12 @@
         inverse_a=((S.RQ, 128), F32),
         inverse_b=((S.RQ, 128), F32),
         mixed=((S.RQ, S.D), F32),
-        base=((EC, S.HE), F32),
-        pre2=((EC, S.HE), F32),
-        G=((EC, S.HE), BF16),
-        upd=((EC, 256), F32),
-        emix=((EC, 256), F32),
+        pre=((EC, S.HM), F32),
+        base=((2, EC, S.HE), F32),
+        pre2=((2, EC, S.HE), F32),
+        G=((2, EC, S.HE), BF16),
+        upd=((2, EC, 256), F32),
+        emix=((2, EC, 256), F32),
         G2=((E, S.HE), BF16),
         DO=((E, 256), BF16),
         DP2=((E, S.HE), BF16),
@@ -1316,6 +1356,12 @@
 STOP = 0
 
 
+def plans(bits):
+    low = list(range(bits - 2))
+    high = [bits - 2, bits - 1]
+    return [low + [-1], low + high, high + low, low + [-1]]
+
+
 def on_device(n_res, *args):
     nodes, edges, neighbours, _, _, _, _, ffn_in = args[:8]
     height = nodes.shape[0]

time: 194 us -> 183 us (0.943)
  Pallas kernels: 193 us -> 182 us
    pallas_call x1, Pallas kernels: 185 us -> 175 us  [on_device(): out = unpack(S, build(S)(*fixed))]
where the time goes in v3:
time: 183 us
  Pallas kernels  182 us (99%)
    pallas_call x1, Pallas kernels, on_device(): out = unpack(S, build(S)(*fixed))  175 us
    pallas_call x1, Pallas kernels, unpack(): pl.pallas_call(body, name='unpack', out_shape=[jax.ShapeDtypeStruct(x, F3...  7.34 us

profile of v3, /device:TPU:0, one launch (start us, length us, event | category | flops | bytes accessed | tf_op | source)
XLA Modules:
  0.0 183.0 jit_solution(14474716916332157196)
XLA Ops:
  0.7 174.8 %layer.1 = (bf16[192,512]{1,0:T(8,128)(2,1)}, bf16[192,6912]{1,0:T(8,128)(2,1)}, f32[48,512]{1,0:T(8,128)}, f32[48,6912]{1,0:T(8,128)}, bf16[2176,128]{1,0:T(8,1...) custom-call(f32[192,512]{1,0:T(8,128)} %refs_0_.1, ...), custom_call_target="tpu_custom_call" | custom-call | tf_op jit(solution)/shard_map/layer/pallas_call | solution.py:1388
  175.5 7.3 %unpack.1 = (f32[192,512]{1,0:T(8,128)}, f32[192,6912]{1,0:T(8,128)}, f32[48,512]{1,0:T(8,128)}, f32[48,6912]{1,0:T(8,128)}, f32[1216,128]{1,0:T(8,128)}, /*inde...) custom-call(bf16[192,512]{1,0:T(8,128)(2,1)} %get-tuple-element.35.r, ...), custom_call_target="tpu_custom_call" | custom-call | tf_op jit(solution)/shard_map/unpack/pallas_call | solution.py:1343

commit v4 on v3

--- a/solution.py
+++ b/solution.py
@@ -56,6 +56,13 @@
 
 def up(rows, step):
     return -(-rows // step) * step
+
+
+def add_step(rows, grain, lanes):
+    parts = rows // grain
+    return grain * max(
+        n for n in range(1, parts + 1) if parts % n == 0 and (n == 1 or n * grain * lanes <= 32768)
+    )
 
 
 def unrolled(count):
@@ -806,9 +813,11 @@
         yield
         a2.wait_recv()
 
-        @pl.loop(0, rows // 32)
+        part = add_step(rows, 16, 128)
+
+        @pl.loop(0, rows // part)
         def _(i):
-            at = rows_at(32 * i, 32)
+            at = rows_at(part * i, part)
             got[1, at] = (g[cross, at].astype(F32) + got[1, at].astype(F32)).astype(BF16)
 
         step = rows // cuts
@@ -822,11 +831,11 @@
         for c in (a1, *pieces):
             c.wait_recv()
 
-        @pl.loop(0, rows // 32)
+        @pl.loop(0, rows // part)
         def _(i):
-            at = rows_at(32 * i, 32)
+            at = rows_at(part * i, part)
             total = g[mp, at].astype(F32) + got[0, at].astype(F32) + got[2, at].astype(F32)
-            work[rows_at(base + 32 * i, 32)] = total.astype(BF16)
+            work[rows_at(base + part * i, part)] = total.astype(BF16)
 
         for c in (a1, a2, *pieces):
             c.wait_send()
@@ -870,12 +879,14 @@
             for c in copies:
                 c.wait()
 
-            @pl.loop(0, size // grain)
-            def _(i, keep=keep, used=used, into=into, terms=len(copies), size=size):
-                at = rows_at(keep + grain * i, grain, grain)
+            step = add_step(size, grain, work.shape[1])
+
+            @pl.loop(0, size // step)
+            def _(i, keep=keep, used=used, into=into, terms=len(copies), size=size, step=step):
+                at = rows_at(keep + step * i, step, grain)
                 total = work[at].astype(F32)
                 for d in range(terms):
-                    total = total + got[rows_at(used + d * size + grain * i, grain, grain)].astype(F32)
+                    total = total + got[rows_at(used + d * size + step * i, step, grain)].astype(F32)
                 into[at] = total.astype(BF16)
 
             used += size * len(copies)
@@ -1000,7 +1011,7 @@
             A.DP[rows] = d
             return total + d.astype(F32)
 
-        total = lax.fori_loop(0, K, back_step, jnp.zeros((16, HM), F32))
+        total = lax.fori_loop(0, K, back_step, jnp.zeros((16, HM), F32), unroll=4)
         A.dmsg_low[16 * sub : 16 * sub + 16] = total.astype(BF16)
 
     move_dmsg = spread_columns(A.dmsg_low, A.dmsg_all)
@@ -1263,11 +1274,7 @@
     stores += [copy(A.eg_l, A.o3), copy(A.ng_l, A.o2)]
 
     def widen(src, dst, out, rows):
-        @pl.loop(0, rows // 16)
-        def _(k):
-            at = pl.ds(pl.multiple_of(16 * k, 16), 16)
-            dst[at] = src[at].astype(F32)
-
+        dst[...] = src[0:rows].astype(F32)
         stores.append(copy(dst, out))
 
     widen(A.i_l, A.i_f, A.o7, D)

time: 183 us -> 182 us (level)
  no operation moved by 1% of the time
where the time goes in v4:
time: 182 us
  Pallas kernels  181 us (99%)
    pallas_call x1, Pallas kernels, on_device(): out = unpack(S, build(S)(*fixed))  174 us
    pallas_call x1, Pallas kernels, unpack(): pl.pallas_call(body, name='unpack', out_shape=[jax.ShapeDtypeStruct(x, F3...  7.34 us

profile of v4, /device:TPU:0, one launch (start us, length us, event | category | flops | bytes accessed | tf_op | source)
XLA Modules:
  0.0 181.8 jit_solution(5063546881323634251)
XLA Ops:
  0.7 173.7 %layer.1 = (bf16[192,512]{1,0:T(8,128)(2,1)}, bf16[192,6912]{1,0:T(8,128)(2,1)}, f32[48,512]{1,0:T(8,128)}, f32[48,6912]{1,0:T(8,128)}, bf16[2176,128]{1,0:T(8,1...) custom-call(f32[192,512]{1,0:T(8,128)} %refs_0_.1, ...), custom_call_target="tpu_custom_call" | custom-call | tf_op jit(solution)/shard_map/layer/pallas_call | solution.py:1395
  174.3 7.3 %unpack.1 = (f32[192,512]{1,0:T(8,128)}, f32[192,6912]{1,0:T(8,128)}, f32[48,512]{1,0:T(8,128)}, f32[48,6912]{1,0:T(8,128)}, f32[1216,128]{1,0:T(8,128)}, /*inde...) custom-call(bf16[192,512]{1,0:T(8,128)(2,1)} %get-tuple-element.35.r, ...), custom_call_target="tpu_custom_call" | custom-call | tf_op jit(solution)/shard_map/unpack/pallas_call | solution.py:1350

commit v5 on v4

--- a/solution.py
+++ b/solution.py
@@ -779,6 +779,8 @@
             at = slice(128 * t, 128 * t + 128)
             emit_edge(t, jnp.transpose(dot_at(A.win3[:, at], A.dq[...])))
         pump(sum_edge)
+
+    def own_edge_gradients():
         landed(move_ds)
         value = dot_at(A.ds_all[...], A.win3[RB : 2 * RB])
         for t in range(4):
@@ -952,6 +954,7 @@
         last_cross.wait_recv()
         on_last.start()
         pump(sum_edge)
+        own_edge_gradients()
 
     d_settled = A.nc_v[...] + dot(A.dself_low[...], A.We[:, 0:D])
     d_settled = d_settled + return_rows(

time: 182 us -> 182 us (level)
  no operation moved by 1% of the time
where the time goes in v5:
time: 182 us
  Pallas kernels  181 us (99%)
    pallas_call x1, Pallas kernels, on_device(): out = unpack(S, build(S)(*fixed))  174 us
    pallas_call x1, Pallas kernels, unpack(): pl.pallas_call(body, name='unpack', out_shape=[jax.ShapeDtypeStruct(x, F3...  7.34 us

profile of v5, /device:TPU:0, one launch (start us, length us, event | category | flops | bytes accessed | tf_op | source)
XLA Modules:
  0.0 181.8 jit_solution(8311098131875144339)
XLA Ops:
  0.7 173.7 %layer.1 = (bf16[192,512]{1,0:T(8,128)(2,1)}, bf16[192,6912]{1,0:T(8,128)(2,1)}, f32[48,512]{1,0:T(8,128)}, f32[48,6912]{1,0:T(8,128)}, bf16[2176,128]{1,0:T(8,1...) custom-call(f32[192,512]{1,0:T(8,128)} %refs_0_.1, ...), custom_call_target="tpu_custom_call" | custom-call | tf_op jit(solution)/shard_map/layer/pallas_call | solution.py:1398
  174.3 7.3 %unpack.1 = (f32[192,512]{1,0:T(8,128)}, f32[192,6912]{1,0:T(8,128)}, f32[48,512]{1,0:T(8,128)}, f32[48,6912]{1,0:T(8,128)}, f32[1216,128]{1,0:T(8,128)}, /*inde...) custom-call(bf16[192,512]{1,0:T(8,128)(2,1)} %get-tuple-element.35.r, ...), custom_call_target="tpu_custom_call" | custom-call | tf_op jit(solution)/shard_map/unpack/pallas_call | solution.py:1353
